TPU v7x, 32 devices: a whole 2x2x4 slice. The times are simulated.
32 devices in a mesh: dp: 2 (over y), ctx: 4 (over x, core), tp: 4 (over z).
Axes of the slice: x: 2, y: 2, z: 4, core: 2. Of those that a mesh axis runs over, the one named last changes fastest.
Arguments:
- layer_input: bfloat16 [2, 2048, 1024], P('dp', 'ctx'), may hold values from -6 to 6
- cotangent: bfloat16 [2, 2048, 1024], P('dp', 'ctx'), may hold values from -6 to 6
- segment_ids: int32 [2, 2048], P('dp'), may hold values from 0 to 11, never falling along the last dimension, each value on 1 to 1536 neighbouring positions
- norm1_gain: bfloat16 [1024], P(('dp', 'ctx')), may hold values from 0.5 to 1.5
- norm1_bias: bfloat16 [1024], P(('dp', 'ctx')), may hold values from -3 to 3
- attend_weight: bfloat16 [1024, 3, 1024], P(('dp', 'ctx'), None, 'tp'), may hold values from -0.1875 to 0.1875
- attend_bias: bfloat16 [2, 1024], P(None, ('tp', 'dp', 'ctx')), may hold values from -3 to 3
- merge_weight: bfloat16 [1024, 1024], P('tp', ('dp', 'ctx')), may hold values from -0.75 to 0.75
- merge_bias: bfloat16 [1024], P(('dp', 'ctx')), may hold values from -3 to 3
- norm2_gain: bfloat16 [1024], P(('dp', 'ctx')), may hold values from 0.5 to 1.5
- norm2_bias: bfloat16 [1024], P(('dp', 'ctx')), may hold values from -3 to 3
- expand_weight: bfloat16 [1024, 4096], P(('dp', 'ctx'), 'tp'), may hold values from -0.1875 to 0.1875
- expand_bias: bfloat16 [4096], P(('tp', 'dp', 'ctx')), may hold values from -3 to 3
- shrink_weight: bfloat16 [4096, 1024], P('tp', ('dp', 'ctx')), may hold values from -0.09375 to 0.09375
- shrink_bias: bfloat16 [1024], P(('dp', 'ctx')), may hold values from -3 to 3
Outputs:
- layer_output: bfloat16 [2, 2048, 1024], P('dp', 'ctx')
- input_grad: bfloat16 [2, 2048, 1024], P('dp', 'ctx')
- grad_norm1_gain: float32 [1024], P(('dp', 'ctx'))
- grad_norm1_bias: float32 [1024], P(('dp', 'ctx'))
- grad_attend_weight: float32 [1024, 3, 1024], P(('dp', 'ctx'), None, 'tp')
- grad_attend_bias: float32 [2, 1024], P(None, ('tp', 'dp', 'ctx'))
- grad_merge_weight: float32 [1024, 1024], P('tp', ('dp', 'ctx'))
- grad_merge_bias: float32 [1024], P(('dp', 'ctx'))
- grad_norm2_gain: float32 [1024], P(('dp', 'ctx'))
- grad_norm2_bias: float32 [1024], P(('dp', 'ctx'))
- grad_expand_weight: float32 [1024, 4096], P(('dp', 'ctx'), 'tp')
- grad_expand_bias: float32 [4096], P(('tp', 'dp', 'ctx'))
- grad_shrink_weight: float32 [4096, 1024], P('tp', ('dp', 'ctx'))
- grad_shrink_bias: float32 [1024], P(('dp', 'ctx'))
Inputs may be any that keep to these rules, and one draw needn't show every extreme that they name: `segment_ids`: within each sequence the segment number never falls; every number 0 to 11 occurs; each holds 1 to 1536 tokens and one holds exactly 1536; segment 0, at the start of a sequence, is padding.
All inputs are finite; a program needn't handle non-finite values.
Results may differ from a plain program's by a relative error of at most 0.02.
Values may be sent and summed in bfloat16 or wider, within the bound.
No kernel may reach another device: no remote copies, remote signals or barrier semaphores. Data moves between devices by JAX's collectives and lax.ppermute only.
A program may use at most 128 MiB of HBM per device.

v0:
```python
import math

import jax
import jax.numpy as jnp
from jax import lax
from jax.sharding import PartitionSpec as P

HD = 64


def norm_forward(values, gain, bias):
    row_mean = jnp.mean(values, axis=-1, keepdims=True)
    centered = values - row_mean
    row_var = jnp.mean(centered * centered, axis=-1, keepdims=True)
    inv_std = lax.rsqrt(row_var + 1e-05)
    normal = centered * inv_std
    return (normal * gain + bias, normal, inv_std)


def norm_backward(grad_out, normal, inv_std, gain):
    grad_normal = grad_out * gain
    centered_grad = grad_normal - jnp.mean(grad_normal, axis=-1, keepdims=True)
    return inv_std * (
        centered_grad - normal * jnp.mean(grad_normal * normal, axis=-1, keepdims=True)
    )


def gelu_tanh(values):
    return (
        0.5
        * values
        * (1.0 + jnp.tanh(0.7978845608028654 * (values + 0.044715 * values * values * values)))
    )


def token_sum(values):
    return jnp.sum(values, axis=(0, 1))


def body(
    layer_input,
    cotangent,
    segment_ids,
    norm1_gain,
    norm1_bias,
    attend_weight,
    attend_bias,
    merge_weight,
    merge_bias,
    norm2_gain,
    norm2_bias,
    expand_weight,
    expand_bias,
    shrink_weight,
    shrink_bias,
):
    fwd_params = (
        lax.all_gather(norm1_gain, ("dp", "ctx"), axis=0, tiled=True),
        lax.all_gather(norm1_bias, ("dp", "ctx"), axis=0, tiled=True),
        lax.all_gather(attend_weight, ("dp", "ctx"), axis=0, tiled=True),
        lax.all_gather(attend_bias, ("dp", "ctx"), axis=1, tiled=True),
        lax.all_gather(merge_weight, ("dp", "ctx"), axis=1, tiled=True),
        lax.all_gather(merge_bias, ("dp", "ctx"), axis=0, tiled=True),
        lax.all_gather(norm2_gain, ("dp", "ctx"), axis=0, tiled=True),
        lax.all_gather(norm2_bias, ("dp", "ctx"), axis=0, tiled=True),
        lax.all_gather(expand_weight, ("dp", "ctx"), axis=0, tiled=True),
        lax.all_gather(expand_bias, ("dp", "ctx"), axis=0, tiled=True),
        lax.all_gather(shrink_weight, ("dp", "ctx"), axis=1, tiled=True),
        lax.all_gather(shrink_bias, ("dp", "ctx"), axis=0, tiled=True),
    )
    gain_one = fwd_params[0].astype(jnp.float32)
    bias_one = fwd_params[1].astype(jnp.float32)
    attention_full_weight = fwd_params[2]
    attend_add = fwd_params[3].astype(jnp.float32)
    merge_full = fwd_params[4]
    merge_add = fwd_params[5].astype(jnp.float32)
    gain_two = fwd_params[6].astype(jnp.float32)
    bias_two = fwd_params[7].astype(jnp.float32)
    expand_full = fwd_params[8]
    expand_add = fwd_params[9].astype(jnp.float32)
    shrink_full = fwd_params[10]
    shrink_add = fwd_params[11].astype(jnp.float32)
    seq_count, q_len, model_width = layer_input.shape
    length = segment_ids.shape[1]
    local_width = attention_full_weight.shape[2]
    heads_local = local_width // HD
    head_scale_factor = 1.0 / math.sqrt(HD)
    ctx_start = lax.axis_index("ctx") * q_len
    inputs = layer_input.astype(jnp.float32)
    norm_out, normal_one, inv_one = norm_forward(inputs, gain_one, bias_one)
    normalized_input = norm_out.astype(jnp.bfloat16)
    projected_rows = jnp.einsum(
        "bhv,vrw->bhrw", normalized_input, attention_full_weight, preferred_element_type=jnp.float32
    )
    query = (projected_rows[:, :, 0] + attend_add[0]).astype(jnp.bfloat16)
    key_local = projected_rows[:, :, 1].astype(jnp.bfloat16)
    value_local = (projected_rows[:, :, 2] + attend_add[1]).astype(jnp.bfloat16)
    keys_all, values_all = (
        lax.all_gather(key_local, "ctx", axis=1, tiled=True),
        lax.all_gather(value_local, "ctx", axis=1, tiled=True),
    )
    seg_query = lax.dynamic_slice_in_dim(segment_ids, ctx_start, q_len, 1)
    query_pos = ctx_start + lax.iota(jnp.int32, q_len)
    key_pos = lax.iota(jnp.int32, length)
    allowed = (seg_query[:, :, None] == segment_ids[:, None, :]) & (
        key_pos[None, None, :] <= query_pos[None, :, None]
    )
    head_outs = []
    lse_list = []
    for head in range(heads_local):
        columns = slice(head * HD, (head + 1) * HD)
        unnormalized_scores = (
            jnp.einsum(
                "sqd,skd->sqk",
                query[..., columns],
                keys_all[..., columns],
                preferred_element_type=jnp.float32,
            )
            * head_scale_factor
        )
        scores = jnp.where(allowed, unnormalized_scores, -1e30)
        row_top = jnp.max(scores, axis=-1, keepdims=True)
        exp_scores = jnp.exp(scores - row_top)
        row_total = jnp.sum(exp_scores, axis=-1, keepdims=True)
        softmax_probabilities = (exp_scores / row_total).astype(jnp.bfloat16)
        head_outs.append(
            jnp.einsum(
                "sqk,skd->sqd",
                softmax_probabilities,
                values_all[..., columns],
                preferred_element_type=jnp.float32,
            )
        )
        lse_list.append(row_top + jnp.log(row_total))
    mixed = jnp.concatenate(head_outs, axis=-1).astype(jnp.bfloat16)
    attn_part = jnp.einsum("sqm,md->sqd", mixed, merge_full, preferred_element_type=jnp.float32)
    attn_out = lax.psum(attn_part.astype(jnp.bfloat16), "tp").astype(jnp.float32)
    hidden = inputs + attn_out + merge_add
    norm_two, normal_two, inv_two = norm_forward(hidden, gain_two, bias_two)
    normed2 = norm_two.astype(jnp.bfloat16)
    pre_act = (
        jnp.einsum("sqd,df->sqf", normed2, expand_full, preferred_element_type=jnp.float32)
        + expand_add
    )
    act_value, gelu_pull = jax.vjp(gelu_tanh, pre_act)
    activation = act_value.astype(jnp.bfloat16)
    mlp_part = jnp.einsum(
        "sqf,fd->sqd", activation, shrink_full, preferred_element_type=jnp.float32
    )
    mlp_out = lax.psum(mlp_part.astype(jnp.bfloat16), "tp").astype(jnp.float32)
    layer_output = (hidden + mlp_out + shrink_add).astype(jnp.bfloat16)
    back_params = (
        lax.all_gather(norm1_gain, ("dp", "ctx"), axis=0, tiled=True),
        lax.all_gather(norm1_bias, ("dp", "ctx"), axis=0, tiled=True),
        lax.all_gather(attend_weight, ("dp", "ctx"), axis=0, tiled=True),
        lax.all_gather(attend_bias, ("dp", "ctx"), axis=1, tiled=True),
        lax.all_gather(merge_weight, ("dp", "ctx"), axis=1, tiled=True),
        lax.all_gather(merge_bias, ("dp", "ctx"), axis=0, tiled=True),
        lax.all_gather(norm2_gain, ("dp", "ctx"), axis=0, tiled=True),
        lax.all_gather(norm2_bias, ("dp", "ctx"), axis=0, tiled=True),
        lax.all_gather(expand_weight, ("dp", "ctx"), axis=0, tiled=True),
        lax.all_gather(expand_bias, ("dp", "ctx"), axis=0, tiled=True),
        lax.all_gather(shrink_weight, ("dp", "ctx"), axis=1, tiled=True),
        lax.all_gather(shrink_bias, ("dp", "ctx"), axis=0, tiled=True),
    )
    gain_one = back_params[0].astype(jnp.float32)
    attention_full_weight = back_params[2]
    merge_full = back_params[4]
    gain_two = back_params[6].astype(jnp.float32)
    expand_full = back_params[8]
    shrink_full = back_params[10]
    keys_all, values_all = (
        lax.all_gather(key_local, "ctx", axis=1, tiled=True),
        lax.all_gather(value_local, "ctx", axis=1, tiled=True),
    )
    keep_mask = (seg_query > 0).astype(jnp.float32)
    grad_y = cotangent.astype(jnp.float32) * keep_mask[:, :, None]
    grad_y_low = grad_y.astype(jnp.bfloat16)
    grad_shrink_w = jnp.einsum(
        "sqf,sqd->fd", activation, grad_y_low, preferred_element_type=jnp.float32
    )
    grad_shrink_b = token_sum(grad_y)
    grad_act = jnp.einsum(
        "sqd,fd->sqf", grad_y_low, shrink_full, preferred_element_type=jnp.float32
    )
    grad_pre = gelu_pull(grad_act)[0].astype(jnp.bfloat16)
    grad_expand_w = jnp.einsum("sqd,sqf->df", normed2, grad_pre, preferred_element_type=jnp.float32)
    grad_expand_b = token_sum(grad_pre.astype(jnp.float32))
    normed2_part = jnp.einsum(
        "sqf,df->sqd", grad_pre, expand_full, preferred_element_type=jnp.float32
    )
    grad_normed2 = lax.psum(normed2_part.astype(jnp.bfloat16), "tp").astype(jnp.float32)
    grad_hidden = grad_y + norm_backward(grad_normed2, normal_two, inv_two, gain_two)
    grad_attn = grad_hidden.astype(jnp.bfloat16)
    grad_norm2_g = token_sum(grad_normed2 * normal_two)
    grad_norm2_b = token_sum(grad_normed2)
    grad_merge_b = token_sum(grad_hidden)
    grad_merge_w = jnp.einsum("sqm,sqd->md", mixed, grad_attn, preferred_element_type=jnp.float32)
    grad_mixed = jnp.einsum(
        "sqd,md->sqm", grad_attn, merge_full, preferred_element_type=jnp.float32
    ).astype(jnp.bfloat16)
    query_grads = []
    key_grads = []
    value_grads = []
    for head in range(heads_local):
        columns = slice(head * HD, (head + 1) * HD)
        query_per_head = query[..., columns]
        key_per_head = keys_all[..., columns]
        value_per_head = values_all[..., columns]
        grad_out_h = grad_mixed[..., columns]
        unnormalized_scores = (
            jnp.einsum(
                "sqd,skd->sqk", query_per_head, key_per_head, preferred_element_type=jnp.float32
            )
            * head_scale_factor
        )
        softmax_f = jnp.where(allowed, jnp.exp(unnormalized_scores - lse_list[head]), 0.0)
        softmax_probabilities = softmax_f.astype(jnp.bfloat16)
        value_grads.append(
            jnp.einsum(
                "sqk,sqd->skd",
                softmax_probabilities,
                grad_out_h,
                preferred_element_type=jnp.float32,
            )
        )
        grad_probs = jnp.einsum(
            "sqd,skd->sqk", grad_out_h, value_per_head, preferred_element_type=jnp.float32
        )
        inner = jnp.sum(softmax_f * grad_probs, axis=-1, keepdims=True)
        grad_scores = (softmax_f * (grad_probs - inner)).astype(jnp.bfloat16)
        query_grads.append(
            jnp.einsum(
                "sqk,skd->sqd", grad_scores, key_per_head, preferred_element_type=jnp.float32
            )
            * head_scale_factor
        )
        key_grads.append(
            jnp.einsum(
                "sqk,sqd->skd", grad_scores, query_per_head, preferred_element_type=jnp.float32
            )
            * head_scale_factor
        )
    grad_query = jnp.concatenate(query_grads, axis=-1).astype(jnp.bfloat16)
    grad_key_sum, grad_value_sum = (
        lax.psum_scatter(
            jnp.concatenate(key_grads, axis=-1).astype(jnp.bfloat16),
            "ctx",
            scatter_dimension=1,
            tiled=True,
        ).astype(jnp.float32),
        lax.psum_scatter(
            jnp.concatenate(value_grads, axis=-1).astype(jnp.bfloat16),
            "ctx",
            scatter_dimension=1,
            tiled=True,
        ).astype(jnp.float32),
    )
    grad_proj = jnp.stack(
        (grad_query, grad_key_sum.astype(jnp.bfloat16), grad_value_sum.astype(jnp.bfloat16)), axis=2
    )
    grad_attend_w = jnp.einsum(
        "sqd,sqcm->dcm", normalized_input, grad_proj, preferred_element_type=jnp.float32
    )
    grad_proj_f = grad_proj.astype(jnp.float32)
    grad_attend_b = jnp.stack(
        (token_sum(grad_proj_f[:, :, 0]), token_sum(grad_proj_f[:, :, 2])), axis=0
    )
    normed1_part = jnp.einsum(
        "sqcm,dcm->sqd", grad_proj, attention_full_weight, preferred_element_type=jnp.float32
    )
    grad_normed1 = lax.psum(normed1_part.astype(jnp.bfloat16), "tp").astype(jnp.float32)
    grad_norm1_g = token_sum(grad_normed1 * normal_one)
    grad_norm1_b = token_sum(grad_normed1)
    input_grad = (grad_hidden + norm_backward(grad_normed1, normal_one, inv_one, gain_one)).astype(
        jnp.bfloat16
    )
    shards = (
        lax.psum_scatter(grad_norm1_g, ("dp", "ctx"), scatter_dimension=0, tiled=True),
        lax.psum_scatter(grad_norm1_b, ("dp", "ctx"), scatter_dimension=0, tiled=True),
        lax.psum_scatter(grad_attend_w, ("dp", "ctx"), scatter_dimension=0, tiled=True),
        lax.psum_scatter(grad_attend_b, ("dp", "ctx"), scatter_dimension=1, tiled=True),
        lax.psum_scatter(grad_merge_w, ("dp", "ctx"), scatter_dimension=1, tiled=True),
        lax.psum_scatter(grad_merge_b, ("dp", "ctx"), scatter_dimension=0, tiled=True),
        lax.psum_scatter(grad_norm2_g, ("dp", "ctx"), scatter_dimension=0, tiled=True),
        lax.psum_scatter(grad_norm2_b, ("dp", "ctx"), scatter_dimension=0, tiled=True),
        lax.psum_scatter(grad_expand_w, ("dp", "ctx"), scatter_dimension=0, tiled=True),
        lax.psum_scatter(grad_expand_b, ("dp", "ctx"), scatter_dimension=0, tiled=True),
        lax.psum_scatter(grad_shrink_w, ("dp", "ctx"), scatter_dimension=1, tiled=True),
        lax.psum_scatter(grad_shrink_b, ("dp", "ctx"), scatter_dimension=0, tiled=True),
    )
    return (
        layer_output,
        input_grad,
        shards[0],
        shards[1],
        shards[2],
        shards[3],
        shards[4],
        shards[5],
        shards[6],
        shards[7],
        shards[8],
        shards[9],
        shards[10],
        shards[11],
    )


def solution(mesh):
    return jax.shard_map(
        body,
        mesh=mesh,
        in_specs=(
            P("dp", "ctx", None),
            P("dp", "ctx", None),
            P("dp", None),
            P(("dp", "ctx")),
            P(("dp", "ctx")),
            P(("dp", "ctx"), None, "tp"),
            P(None, ("tp", "dp", "ctx")),
            P("tp", ("dp", "ctx")),
            P(("dp", "ctx")),
            P(("dp", "ctx")),
            P(("dp", "ctx")),
            P(("dp", "ctx"), "tp"),
            P(("tp", "dp", "ctx")),
            P("tp", ("dp", "ctx")),
            P(("dp", "ctx")),
        ),
        out_specs=(
            P("dp", "ctx", None),
            P("dp", "ctx", None),
            P(("dp", "ctx")),
            P(("dp", "ctx")),
            P(("dp", "ctx"), None, "tp"),
            P(None, ("tp", "dp", "ctx")),
            P("tp", ("dp", "ctx")),
            P(("dp", "ctx")),
            P(("dp", "ctx")),
            P(("dp", "ctx")),
            P(("dp", "ctx"), "tp"),
            P(("tp", "dp", "ctx")),
            P("tp", ("dp", "ctx")),
            P(("dp", "ctx")),
        ),
        check_vma=False,
    )
```

profile of v0, /device:TPU:0, one launch (start us, length us, event | category | flops | bytes accessed | tf_op | source)
XLA Modules:
  0.0 676.4 jit_solution(15304905114799007541)
XLA Ops:
  9.1 10.3 %all-gather.1 = bf16[8,1,128]{2,1,0:T(2,128)(2,1)S(1)} all-gather(bf16[1,1,128]{2,1,0:T(2,128)(2,1)} %bitcast.294), channel_id=1, replica_groups=mesh['dp'=2,'ctx'=4,'tp'=4] {'dp','ctx'}, dimensions={0}, use_global_device_ids=true | all-gather | bytes 2304 | tf_op jit(solution)/shard_map/all_gather | solution.py:58
  19.4 8.6 %all-gather.2 = bf16[8,1,128]{2,1,0:T(2,128)(2,1)S(1)} all-gather(bf16[1,1,128]{2,1,0:T(2,128)(2,1)} %bitcast.295), channel_id=1, replica_groups=mesh['dp'=2,'ctx'=4,'tp'=4] {'dp','ctx'}, dimensions={0}, use_global_device_ids=true | all-gather | bytes 2304 | tf_op jit(solution)/shard_map/all_gather | solution.py:59
  30.0 9.1 %all-gather.15.cloned.1.call-done = bf16[1024,3,256]{0,2,1:T(8,128)(2,1)} async-done(((bf16[128,3,256]{0,2,1:T(8,128)(2,1)}), bf16[1024,3,256]{0,2,1:T(8,128)(2,1)}) %all-gather.15.cloned.1.call-update) | async-done | bytes 1572880 | tf_op jit(solution)/shard_map/all_gather | solution.py:60
  43.7 8.7 %all-gather.3 = bf16[8,32,2]{1,2,0:T(2,128)(2,1)S(1)} all-gather(bf16[1,32,2]{1,2,0:T(2,128)(2,1)S(1)} %bitcast.296), channel_id=1, replica_groups=mesh['dp'=2,'ctx'=4,'tp'=4] {'dp','ctx'}, dimensions={0}, use_global_device_ids=true | all-gather | bytes 1152 | tf_op jit(solution)/shard_map/all_gather | solution.py:61
  52.6 9.8 %all_gather.56 = bf16[256,1024]{1,0:T(8,128)(2,1)S(1)} all-gather(bf16[256,128]{1,0:T(8,128)(2,1)S(1)} %copy-done.43), channel_id=1, replica_groups=mesh['dp'=2,'ctx'=4,'tp'=4] {'dp','ctx'}, dimensions={1}, use_global_device_ids=true | all-gather | bytes 589824 | tf_op jit(solution)/shard_map/all_gather | solution.py:62
  73.6 4.5 fusion.2
  81.4 4.0 fusion.72
  94.4 8.7 %all-gather.4 = bf16[8,1,128]{2,1,0:T(2,128)(2,1)S(1)} all-gather(bf16[1,1,128]{2,1,0:T(2,128)(2,1)S(1)} %bitcast.297), channel_id=1, replica_groups=mesh['dp'=2,'ctx'=4,'tp'=4] {'dp','ctx'}, dimensions={0}, use_global_device_ids=true | all-gather | bytes 2304 | tf_op jit(solution)/shard_map/all_gather | solution.py:63
  103.1 7.8 %all-gather.5 = bf16[8,1,128]{2,1,0:T(2,128)(2,1)S(1)} all-gather(bf16[1,1,128]{2,1,0:T(2,128)(2,1)S(1)} %bitcast.298), channel_id=1, replica_groups=mesh['dp'=2,'ctx'=4,'tp'=4] {'dp','ctx'}, dimensions={0}, use_global_device_ids=true | all-gather | bytes 2304 | tf_op jit(solution)/shard_map/all_gather | solution.py:64
  110.9 8.7 %all-gather.6 = bf16[8,1,128]{2,1,0:T(2,128)(2,1)S(1)} all-gather(bf16[1,1,128]{2,1,0:T(2,128)(2,1)S(1)} %bitcast.299), channel_id=1, replica_groups=mesh['dp'=2,'ctx'=4,'tp'=4] {'dp','ctx'}, dimensions={0}, use_global_device_ids=true | all-gather | bytes 2304 | tf_op jit(solution)/shard_map/all_gather | solution.py:65
  119.6 8.3 %all-gather.7 = bf16[8,1,128]{2,1,0:T(2,128)(2,1)S(1)} all-gather(bf16[1,1,128]{2,1,0:T(2,128)(2,1)S(1)} %bitcast.300), channel_id=1, replica_groups=mesh['dp'=2,'ctx'=4,'tp'=4] {'dp','ctx'}, dimensions={0}, use_global_device_ids=true | all-gather | bytes 2304 | tf_op jit(solution)/shard_map/all_gather | solution.py:67
  127.9 17.2 %all-reduce.13.cloned.1.call-done = bf16[1,512,1024]{2,1,0:T(8,128)(2,1)} async-done(((bf16[1,512,1024]{2,1,0:T(8,128)(2,1)}), bf16[1,512,1024]{2,1,0:T(8,128)(2,1)}) %all-reduce.13.cloned.1.call-update) | async-done | bytes 1048592 | tf_op jit(solution)/shard_map/psum | solution.py:137
  147.5 26.9 %all-gather.19.cloned.1.call-done = bf16[1024,1024]{1,0:T(8,128)(2,1)} async-done(((bf16[128,1024]{1,0:T(8,128)(2,1)}), bf16[1024,1024]{1,0:T(8,128)(2,1)}) %all-gather.19.cloned.1.call-update) | async-done | bytes 2097168 | tf_op jit(solution)/shard_map/all_gather | solution.py:66
  174.3 4.3 fusion.121
  178.6 25.9 %all-gather.21.cloned.1.call-done = bf16[1024,1024]{1,0:T(8,128)(2,1)} async-done(((bf16[1024,128]{1,0:T(8,128)(2,1)}), bf16[1024,1024]{1,0:T(8,128)(2,1)}) %all-gather.21.cloned.1.call-update) | async-done | bytes 2097168 | tf_op jit(solution)/shard_map/all_gather | solution.py:68
  204.4 6.1 convert_reduce_fusion.3
  214.1 51.7 %all-reduce.15.cloned.1.call-done = bf16[1,512,1024]{2,1,0:T(8,128)(2,1)} async-done(((bf16[1,512,1024]{2,1,0:T(8,128)(2,1)}), bf16[1,512,1024]{2,1,0:T(8,128)(2,1)}) %all-reduce.15.cloned.1.call-update) | async-done | bytes 1048592 | tf_op jit(solution)/shard_map/psum | solution.py:192
  291.3 9.1 %multiply_reduce_fusion.3 = (f32[512]{0:T(512)S(1)}, f32[512]{0:T(512)S(1)}, f32[512]{0:T(512)S(1)}, f32[512]{0:T(512)S(1)}, f32[512,2048]{1,0:T(8,128)}) fusion(f32[512]{0:T(512)S(1)} %get-tuple-element.68, f32[512,2048]{1,0:T(8,128)} %copy-done.22, s32[512]{0:T(512)S(1)} %iota_add_fusion, s32[2048]{0:T(1024)S(1)} %bitcast.254, s32[512]{0:T(512)S(1)} %bitcast.275, ...), kind=kOutput, calls=%fused_computation.10 | convolution fusion | flops 158332928 | bytes 33910784 | tf_op jit(solution)/shard_map/sqd,skd->sqk/dot_general | solution.py:227
  300.4 13.1 %multiply_convert_fusion.3 = (bf16[512,2048]{1,0:T(8,128)(2,1)}, bf16[512,2048]{1,0:T(8,128)(2,1)}, bf16[512,2048]{1,0:T(8,128)(2,1)}, bf16[512,2048]{1,0:T(8,128)(2,1)}) fusion(f32[512,2048]{1,0:T(8,128)} %get-tuple-element.62, f32[512]{0:T(512)S(1)} %get-tuple-element.24, f32[512]{0:T(512)S(1)} %get-tuple-element.68, f32[512,2048]{1,0:T(8,128)} %copy-done.22, ...), kind=kLoop, calls=%fused_computation.9 | loop fusion | flops 28311552 | bytes 41971712 | tf_op jit(solution)/shard_map/convert_element_type | solution.py:231
  319.1 4.8 fusion.64
  327.8 15.7 %reduce-scatter.10.cloned.1.call-done = bf16[1,512,256]{1,2,0:T(8,128)(2,1)} async-done(((bf16[1,2048,256]{1,2,0:T(8,128)(2,1)}), bf16[1,512,256]{1,2,0:T(8,128)(2,1)}) %reduce-scatter.10.cloned.1.call-update) | async-done | bytes 262160 | tf_op jit(solution)/shard_map/reduce_scatter | solution.py:246
  353.4 5.6 fusion.90
  359.1 5.0 fusion.119
  364.7 3.9 fusion.114
  369.3 8.6 %all-gather.8 = bf16[8,1,128]{2,1,0:T(2,128)(2,1)S(1)} all-gather(bf16[1,1,128]{2,1,0:T(2,128)(2,1)S(1)} %bitcast.301), channel_id=1, replica_groups=mesh['dp'=2,'ctx'=4,'tp'=4] {'dp','ctx'}, dimensions={0}, use_global_device_ids=true | all-gather | bytes 2304 | tf_op jit(solution)/shard_map/all_gather | solution.py:69
  381.1 88.9 %all-reduce.17.cloned.1.call-done = (bf16[1,512,1024]{2,1,0:T(8,128)(2,1)}, bf16[1,512,1024]{2,1,0:T(8,128)(2,1)}) async-done(((bf16[1,512,1024]{2,1,0:T(8,128)(2,1)}, bf16[1,512,1024]{2,1,0:T(8,128)(2,1)}), (bf16[1,512,1024]{2,1,0:T(8,128)(2,1)}, bf16[1,512,1024]{2,1,0:T(8,128)(2,1)})) %all-reduce.17.cloned.1.call-update) | async-done | bytes 2097168 | tf_op jit(solution)/shard_map/psum | solution.py:150
  472.3 24.2 %all-reduce.7 = (f32[1024]{0:T(1024)S(1)}, f32[1024]{0:T(1024)S(1)}, f32[1024]{0:T(1024)S(1)}, f32[1024]{0:T(1024)S(1)}, f32[1024]{0:T(1024)S(1)}, /*index=5*/f32[1024]{0:T(1024)S(1)}, f32[1024]{0:T(1024)S(1)}) all-reduce(f32[1024]{0:T(1024)S(1)} %get-tuple-element.16, ...), channel_id=5, replica_groups=mesh['dp'=2,'ctx'=4,'tp'=4] {'dp','ctx'}, use_global_device_ids=true, to_apply=%region_27.28.clone | all-reduce | flops 7168 | bytes 57344
  500.5 3.6 fusion.36
  504.1 4.5 reduce-scatter.16.cloned.1.call-done
  508.6 55.3 %reduce-scatter.20.cloned.1.call-done = f32[1024,128]{1,0:T(8,128)} async-done(((f32[1024,1024]{1,0:T(8,128)}), f32[1024,128]{1,0:T(8,128)}) %reduce-scatter.20.cloned.1.call-update) | async-done | bytes 524304 | tf_op jit(solution)/shard_map/reduce_scatter | solution.py:289
  563.9 55.5 %reduce-scatter.18.cloned.1.call-done = f32[128,1024]{1,0:T(8,128)} async-done(((f32[1024,1024]{1,0:T(8,128)}), f32[128,1024]{1,0:T(8,128)}) %reduce-scatter.18.cloned.1.call-update) | async-done | bytes 524304 | tf_op jit(solution)/shard_map/reduce_scatter | solution.py:287
  619.4 50.1 %reduce-scatter.14.cloned.1.call-done = f32[128,3,256]{2,0,1:T(8,128)} async-done(((f32[1024,3,256]{2,0,1:T(8,128)}), f32[128,3,256]{2,0,1:T(8,128)}) %reduce-scatter.14.cloned.1.call-update) | async-done | bytes 393232 | tf_op jit(solution)/shard_map/reduce_scatter | solution.py:281
  (243 shorter events, 92.1 us)
Async XLA Ops:
  7.2 22.3 %copy-start.7 = (bf16[1,512,1024]{2,1,0:T(8,128)(2,1)S(1)}, bf16[1,512,1024]{2,1,0:T(8,128)(2,1)}, u32[]{:S(2)}) copy-start(bf16[1,512,1024]{2,1,0:T(8,128)(2,1)} %param.15) | copy-start | bytes 3145732
  7.2 31.9 %all-gather.15.cloned.1.call-start = ((), (), s32[]{:S(2)}) async-start(), calls=%async_computation.7 | async-start | bytes 1769472 | tf_op jit(solution)/shard_map/all_gather | solution.py:60
  9.1 55.4 %all-gather.23.cloned.1.call-start = ((), (), s32[]{:S(2)}) async-start(), calls=%async_computation.19 | async-start | bytes 1310720 | tf_op jit(solution)/shard_map/all_gather | solution.py:99
  28.1 13.7 %copy-start.55 = (f32[8,1,128]{2,1,0:T(1,128)}, f32[8,1,128]{2,1,0:T(1,128)S(1)}, u32[]{:S(2)}) copy-start(f32[8,1,128]{2,1,0:T(1,128)S(1)} %convert_element_type.298) | copy-start | bytes 12292
  43.7 37.7 %all-gather.17.cloned.1.call-start = ((), (), s32[]{:S(2)}) async-start(), calls=%async_computation.8 | async-start | bytes 1310720 | tf_op jit(solution)/shard_map/all_gather | solution.py:100
  52.6 216.4 %copy-start.53 = (f32[1,512]{1,0:T(1,128)}, f32[1,512]{1,0:T(1,128)S(1)}, u32[]{:S(2)}) copy-start(f32[1,512]{1,0:T(1,128)S(1)} %get-tuple-element.46) | copy-start | bytes 6148
  64.5 80.7 %all-reduce.13.cloned.1.call-start = ((), (), s32[]{:S(2)}) async-start(), calls=%async_computation.9 | async-start | bytes 2097152 | tf_op jit(solution)/shard_map/psum | solution.py:137
  91.6 55.2 %copy-start.41 = (bf16[512,64]{0,1:T(8,128)(2,1)}, bf16[512,64]{0,1:T(8,128)(2,1)S(1)}, u32[]{:S(2)}) copy-start(bf16[512,64]{0,1:T(8,128)(2,1)S(1)} %fusion.73) | copy-start | bytes 196612
  91.6 19.2 %copy-start.61 = (bf16[128]{0:T(256)(128)(2,1)S(1)}, bf16[128]{0:T(256)(128)(2,1)}, u32[]{:S(2)}) copy-start(bf16[128]{0:T(256)(128)(2,1)} %param.25) | copy-start | bytes 772
  91.7 27.9 %copy-start.62 = (bf16[128]{0:T(256)(128)(2,1)S(1)}, bf16[128]{0:T(256)(128)(2,1)}, u32[]{:S(2)}) copy-start(bf16[128]{0:T(256)(128)(2,1)} %param.27) | copy-start | bytes 772
  93.1 81.2 %all-gather.19.cloned.1.call-start = ((), (), s32[]{:S(2)}) async-start(), calls=%async_computation.10 | async-start | bytes 2359296 | tf_op jit(solution)/shard_map/all_gather | solution.py:66
  93.7 110.7 %all-gather.21.cloned.1.call-start = ((), (), s32[]{:S(2)}) async-start(), calls=%async_computation.11 | async-start | bytes 2359296 | tf_op jit(solution)/shard_map/all_gather | solution.py:68
  94.3 171.5 %all-reduce.15.cloned.1.call-start = ((), (), s32[]{:S(2)}) async-start(), calls=%async_computation.12 | async-start | bytes 2097152 | tf_op jit(solution)/shard_map/psum | solution.py:192
  119.6 54.8 %copy-start.56 = (f32[8,1,128]{2,1,0:T(1,128)}, f32[8,1,128]{2,1,0:T(1,128)S(1)}, u32[]{:S(2)}) copy-start(f32[8,1,128]{2,1,0:T(1,128)S(1)} %convert_element_type.302) | copy-start | bytes 12292
  127.9 191.2 %copy-start.57 = (f32[8,1,128]{2,1,0:T(1,128)}, f32[8,1,128]{2,1,0:T(1,128)S(1)}, u32[]{:S(2)}) copy-start(f32[8,1,128]{2,1,0:T(1,128)S(1)} %convert_element_type.303) | copy-start | bytes 12292
  147.4 121.6 %copy-start.46 = (f32[512]{0:T(512)}, f32[512]{0:T(512)S(1)}, u32[]{:S(2)}) copy-start(f32[512]{0:T(512)S(1)} %add_rsqrt_fusion) | copy-start | bytes 6148
  213.9 113.9 %reduce-scatter.12.cloned.1.call-start = ((), (), s32[]{:S(2)}) async-start(), calls=%async_computation.14 | async-start | bytes 1310720 | tf_op jit(solution)/shard_map/reduce_scatter | solution.py:252
  281.5 61.9 %reduce-scatter.10.cloned.1.call-start = ((), (), s32[]{:S(2)}) async-start(), calls=%async_computation.13 | async-start | bytes 1310720 | tf_op jit(solution)/shard_map/reduce_scatter | solution.py:246
  319.0 60.7 %reduce-scatter.22.cloned.1.call-start = ((), (), s32[]{:S(2)}) async-start(), calls=%async_computation.20 | async-start | bytes 147456
  327.8 18.2 %copy-start.32 = (bf16[1,512,256]{1,2,0:T(8,128)(2,1)S(1)}, bf16[1,512,256]{1,2,0:T(8,128)(2,1)}, u32[]{:S(2)}) copy-start(bf16[1,512,256]{1,2,0:T(8,128)(2,1)} %reduce-scatter.12.cloned.1.call-done) | copy-start | bytes 786436
  327.8 18.2 %copy-start.35 = (bf16[512,64]{0,1:T(8,128)(2,1)S(1)}, bf16[512,64]{0,1:T(8,128)(2,1)}, u32[]{:S(2)}) copy-start(bf16[512,64]{0,1:T(8,128)(2,1)} %copy-done.34) | copy-start | bytes 196612
  327.8 18.2 %copy-start.37 = (bf16[512,64]{0,1:T(8,128)(2,1)S(1)}, bf16[512,64]{0,1:T(8,128)(2,1)}, u32[]{:S(2)}) copy-start(bf16[512,64]{0,1:T(8,128)(2,1)} %copy-done.36) | copy-start | bytes 196612
  345.6 124.3 %all-reduce.17.cloned.1.call-start = ((), (), s32[]{:S(2)}) async-start(), calls=%async_computation.21 | async-start | bytes 4194304 | tf_op jit(solution)/shard_map/psum | solution.py:150
  349.4 159.2 %reduce-scatter.16.cloned.1.call-start = ((), (), s32[]{:S(2)}) async-start(), calls=%async_computation.16 | async-start | bytes 1179648 | tf_op jit(solution)/shard_map/reduce_scatter | solution.py:283
  353.3 210.5 %reduce-scatter.20.cloned.1.call-start = ((), (), s32[]{:S(2)}) async-start(), calls=%async_computation.18 | async-start | bytes 4718592 | tf_op jit(solution)/shard_map/reduce_scatter | solution.py:289
  359.1 260.3 %reduce-scatter.18.cloned.1.call-start = ((), (), s32[]{:S(2)}) async-start(), calls=%async_computation.17 | async-start | bytes 4718592 | tf_op jit(solution)/shard_map/reduce_scatter | solution.py:287
  364.1 305.4 %reduce-scatter.14.cloned.1.call-start = ((), (), s32[]{:S(2)}) async-start(), calls=%async_computation.15 | async-start | bytes 3538944 | tf_op jit(solution)/shard_map/reduce_scatter | solution.py:281
  368.7 103.5 %copy-start.49 = (f32[1024]{0:T(1024)S(1)}, f32[1024]{0:T(1024)}, u32[]{:S(2)}) copy-start(f32[1024]{0:T(1024)} %get-tuple-element.14) | copy-start | bytes 12292
  368.7 103.5 %copy-start.50 = (f32[1024]{0:T(1024)S(1)}, f32[1024]{0:T(1024)}, u32[]{:S(2)}) copy-start(f32[1024]{0:T(1024)} %get-tuple-element.22) | copy-start | bytes 12292
  368.7 103.5 %copy-start.51 = (f32[1024]{0:T(1024)S(1)}, f32[1024]{0:T(1024)}, u32[]{:S(2)}) copy-start(f32[1024]{0:T(1024)} %get-tuple-element.44) | copy-start | bytes 12292
  368.7 103.5 %copy-start.52 = (f32[1024]{0:T(1024)S(1)}, f32[1024]{0:T(1024)}, u32[]{:S(2)}) copy-start(f32[1024]{0:T(1024)} %get-tuple-element.50) | copy-start | bytes 12292
  368.7 103.5 %copy-start.54 = (f32[1024]{0:T(1024)S(1)}, f32[1024]{0:T(1024)}, u32[]{:S(2)}) copy-start(f32[1024]{0:T(1024)} %get-tuple-element.63) | copy-start | bytes 12292
  (50 other events, 209.3 us)
Sparse Core Ops, SparseCore 0:
  10.5 28.5 all-gather.14
  43.8 17.5 all-gather.22
  64.6 16.7 all-gather.16
  93.2 51.8 all-reduce.12
  147.0 27.2 all-gather.18
  176.2 28.1 all-gather.20
  214.0 51.7 all-reduce.14
  281.6 24.2 reduce-scatter.11
  319.2 24.2 reduce-scatter.9
  346.3 33.4 reduce-scatter.21
  382.9 87.0 all-reduce.16
  473.6 34.9 reduce-scatter.15
  512.5 51.2 reduce-scatter.19
  568.0 51.3 reduce-scatter.17
  623.2 46.2 reduce-scatter.13
where the time goes:
time: 684 us; the launch traced here: 676 us
  waiting for transfers between devices  406 us (59%)
  blocking collectives  104 us (15%)
  matrix products  86.7 us (13%)
  other arithmetic  38.4 us (6%)
  local copies, waits for them, and re-layouts  24.8 us (4%)
  between operations  15.8 us (2%)
    psum x1, waiting for transfers between devices, body(): mlp_out = lax.psum(mlp_part.astype(jnp.bfloat16), 'tp').astype(jnp.float32)  88.9 us
    reduce_scatter x1, waiting for transfers between devices, body(): lax.psum_scatter(grad_expand_w, ('dp', 'ctx'), scatter_dimension=0, tiled...  55.5 us
    reduce_scatter x1, waiting for transfers between devices, body(): lax.psum_scatter(grad_shrink_w, ('dp', 'ctx'), scatter_dimension=1, tiled...  55.3 us
    psum x1, waiting for transfers between devices, body(): lax.psum(normed2_part.astype(jnp.bfloat16), 'tp').astype(jnp.float32)  51.7 us
    reduce_scatter x1, waiting for transfers between devices, body(): lax.psum_scatter(grad_attend_w, ('dp', 'ctx'), scatter_dimension=0, tiled...  50.1 us
    all_gather x1, waiting for transfers between devices, body(): lax.all_gather(expand_weight, ('dp', 'ctx'), axis=0, tiled=True)  26.9 us
    all_gather x1, waiting for transfers between devices, body(): lax.all_gather(shrink_weight, ('dp', 'ctx'), axis=1, tiled=True)  25.9 us
    unnamed x1, blocking collectives  24.2 us
  transfers between devices with their start and end apart: 15, of which 13 were waited for; matrix products, arithmetic and copies ran while one was open for 14% of the time, Pallas kernels for 0%

commit v1 on v0

v1 whole, which is shorter than its diff:
```python
import functools

import jax
import jax.numpy as jnp
from jax import lax
from jax.experimental import pallas as pl
from jax.experimental.pallas import tpu as pltpu
from jax.sharding import PartitionSpec as P

HD = 64
NEG = -1e30
F32 = jnp.float32
BF16 = jnp.bfloat16


def dot(left, right, left_dim, right_dim):
    return lax.dot_general(
        left, right, (((left_dim,), (right_dim,)), ((), ())), preferred_element_type=F32
    )


def shape(dims, dtype):
    return jax.ShapeDtypeStruct(tuple(dims), dtype)


def call(kernel, name, scalars, ins, outs, scratch=(), flops=0):
    first = [] if scalars is None else [scalars]
    specs, arrays, moved = [], [], 0
    for value in ins:
        if isinstance(value, tuple):
            value, dims, index = value
            specs.append(pl.BlockSpec(dims, lambda i, index=index: index))
            moved += value.dtype.itemsize * functools.reduce(lambda a, b: a * b, dims)
        else:
            specs.append(pl.BlockSpec(memory_space=pltpu.VMEM))
            moved += value.size * value.dtype.itemsize
        arrays.append(value)
    moved += sum(v.size * v.dtype.itemsize for v in outs)
    return pl.pallas_call(
        kernel,
        grid=(1,),
        out_shape=tuple(outs),
        in_specs=[pl.BlockSpec(memory_space=pltpu.SMEM)] * len(first) + specs,
        out_specs=(pl.BlockSpec(memory_space=pltpu.VMEM),) * len(outs),
        scratch_shapes=list(scratch),
        compiler_params=pltpu.CompilerParams(vmem_limit_bytes=56 << 20),
        cost_estimate=pl.CostEstimate(
            flops=flops, transcendentals=0, bytes_accessed=moved
        ),
        name=name,
    )(*first, *arrays)


def lanes(index, offset, size):
    return pl.ds(pl.multiple_of((index ^ offset) * size, size), size)


def rows_of(refs, low, high):
    return jnp.concatenate([ref[low:high, :] for ref in refs], axis=0)


def pack_kernel(attend_ref, *refs):
    smalls, (pair_ref, out_ref) = refs[:-2], refs[-2:]
    parts, block, width = attend_ref.shape
    for c in range(parts):
        out_ref[:block, c * width : (c + 1) * width] = attend_ref[c]
    size = smalls[0].shape[1]
    last = jnp.concatenate([pair_ref[0:1, :], pair_ref[1:2, :]], axis=1).astype(F32)
    last = jnp.concatenate([last, jnp.zeros((1, size - last.shape[1]), F32)], axis=1)
    rows = jnp.concatenate([ref[...].astype(F32) for ref in smalls] + [last], axis=0)
    out_ref[block:, :size] = rows.astype(BF16)
    out_ref[block:, size:] = jnp.zeros((8, parts * width - size), BF16)


def turn_kernel(expand_ref, shrink_ref, *refs):
    parts, out_ref = refs[:-1], refs[-1]
    block = expand_ref.shape[0]
    out_ref[:block, :] = expand_ref[...]
    out_ref[block : 2 * block, :] = shrink_ref[...].T
    width = parts[0].shape[0]
    for o, ref in enumerate(parts):
        out_ref[2 * block :, o * width : (o + 1) * width] = ref[...].T


def decode(order, head_block, index, first, start, size, wide_ref, expand_ref, attend_ref):
    total = jnp.zeros(attend_ref.shape, F32)
    for place, offset in enumerate(order):
        rows = first[place][start : start + 8, :size].astype(F32)
        wide_ref[:, place * size : (place + 1) * size] = rows
        expand_ref[:, lanes(index, offset, size)] = rows[6:7, :]
        flat = jnp.concatenate([rows[7:8, :head_block], rows[7:8, head_block : 2 * head_block]], 0)
        flat = jnp.concatenate(
            [flat, jnp.zeros((2, attend_ref.shape[1] - head_block), F32)], axis=1
        )
        flat = jnp.concatenate([flat, jnp.zeros((6, attend_ref.shape[1]), F32)], axis=0)
        total = total + pltpu.roll(flat, (index ^ offset) * head_block, 1)[:2]
    attend_ref[...] = total


def grad_order_kernel(order, count, scalars, cot_ref, keep_ref, *outs):
    index, tp = scalars[0], scalars[2]
    height, wide = outs[0].shape
    size = wide // len(order)
    for o in range(count):
        rows = pl.ds(pl.multiple_of((tp ^ o) * height, height), height)
        keep = keep_ref[rows, 0:1]
        for place, offset in enumerate(order):
            outs[o][:, place * size : (place + 1) * size] = (
                cot_ref[rows, lanes(index, offset, size)] * keep
            )


def project_kernel(order, block, head_block, scalars, x_ref, *refs):
    count = len(order)
    weights, refs = refs[:count], refs[count:]
    given, outs = refs[:-7], refs[-7:]
    normed_ref, query_ref, pair_ref, rows_ref = outs[:4]
    wide_ref, expand_ref, attend_ref = outs[4:]
    index, tp = scalars[0], scalars[2]
    q_len, wide = x_ref.shape
    size = wide // count
    for source, target in zip(given, outs[4:]):
        target[...] = source[...]
    if not given:
        decode(order, head_block, index, weights, block, size, wide_ref, expand_ref, attend_ref)
    width = query_ref.shape[1]
    weight = rows_of(weights, 0, block)
    step = min(q_len, 256)
    bias = jnp.concatenate(
        [attend_ref[0:1, :], jnp.zeros((1, width), F32), attend_ref[1:2, :]], axis=1
    )
    for start in range(0, q_len, step):
        rows = slice(start, start + step)
        value = x_ref[rows, :].astype(F32)
        mean = jnp.mean(value, axis=-1, keepdims=True)
        centered = value - mean
        inv = lax.rsqrt(jnp.mean(centered * centered, axis=-1, keepdims=True) + 1e-05)
        for place, offset in enumerate(order):
            plain = slice(place * size, (place + 1) * size)
            part = x_ref[rows, lanes(index, offset, size)].astype(F32)
            part = (part - mean) * inv * wide_ref[0:1, plain] + wide_ref[1:2, plain]
            normed_ref[rows, plain] = part.astype(BF16)
        made = dot(normed_ref[rows, :], weight, 1, 0) + bias
        query_ref[rows, :] = made[:, :width].astype(BF16)
        pair_ref[rows, :] = made[:, width:].astype(BF16)
    height = rows_ref.shape[0]
    mine = pl.ds(pl.multiple_of(tp * height, height), height)
    for place, offset in enumerate(order):
        plain = slice(place * size, (place + 1) * size)
        rows_ref[:, plain] = x_ref[mine, lanes(index, offset, size)]


def attend_kernel(heads, tq, tk, n_chunk, n_tp, scalars, lo_ref, q_ref, *refs):
    kv_refs = refs[:n_chunk]
    outs, refs = refs[n_chunk : n_chunk + n_tp], refs[n_chunk + n_tp :]
    lse_ref, qm_ref, acc_ref, m_ref, l_ref, mixed_ref = refs
    q_len, width = q_ref.shape
    ctx = scalars[1]
    lane = lax.broadcasted_iota(jnp.int32, (tq, width), 1)
    for qi in range(q_len // tq):
        rows = slice(qi * tq, (qi + 1) * tq)
        qv = q_ref[rows, :] * BF16(0.125)
        for h in range(heads):
            mine = (lane >= h * HD) & (lane < (h + 1) * HD)
            qm_ref[h] = jnp.where(mine, qv, jnp.zeros_like(qv))
        acc_ref[...] = jnp.zeros_like(acc_ref)
        m_ref[...] = jnp.full(m_ref.shape, NEG, F32)
        l_ref[...] = jnp.zeros_like(l_ref)
        qbase = ctx * q_len + qi * tq
        qpos = qbase + lax.broadcasted_iota(jnp.int32, (1, tq), 1)
        lo = lo_ref[0:1, rows]
        lo_first = scalars[3 + qi]
        for c in range(n_chunk):
            kv = kv_refs[c]
            cbase = (ctx ^ c) * q_len

            def step(ki, carry, kv=kv, cbase=cbase):
                kb = cbase + ki * tk

                @pl.when((kb <= qbase + tq - 1) & (kb + tk - 1 >= lo_first))
                def _():
                    krows = pl.ds(pl.multiple_of(ki * tk, tk), tk)
                    k = kv[krows, 0:width]
                    vt = kv[krows, width : 2 * width].T
                    kpos = kb + lax.broadcasted_iota(jnp.int32, (tk, 1), 0)
                    ok = (kpos >= lo) & (kpos <= qpos)
                    for h in range(heads):
                        s = jnp.where(ok, dot(k, qm_ref[h], 1, 1), NEG)
                        m0 = m_ref[h : h + 1, :]
                        m1 = jnp.maximum(m0, jnp.max(s, axis=0, keepdims=True))
                        p = jnp.exp(s - m1)
                        al = jnp.exp(m0 - m1)
                        l_ref[h : h + 1, :] = l_ref[h : h + 1, :] * al + jnp.sum(
                            p, axis=0, keepdims=True
                        )
                        m_ref[h : h + 1, :] = m1
                        hs = slice(h * HD, (h + 1) * HD)
                        acc_ref[hs, :] = acc_ref[hs, :] * al + dot(
                            vt[hs, :], p.astype(BF16), 1, 0
                        )

                return carry

            lax.fori_loop(0, q_len // tk, step, 0)
        lse_ref[:, rows] = m_ref[0:heads, :] + jnp.log(l_ref[0:heads, :])
        for h in range(heads):
            hs = slice(h * HD, (h + 1) * HD)
            acc_ref[hs, :] = acc_ref[hs, :] / l_ref[h : h + 1, :]
        mixed_ref[rows, :] = acc_ref[...].T.astype(BF16)
    for o in range(n_tp):
        outs[o][...] = mixed_ref[lanes(scalars[2], o, q_len // n_tp), :]


def attend_back_kernel(heads, tq, tk, n_chunk, n_tp, scalars, lo_ref, lse_ref, q_ref, *refs):
    kv_refs, refs = refs[:n_chunk], refs[n_chunk:]
    mixed_refs, refs = refs[:n_tp], refs[n_tp:]
    gm_refs, refs = refs[:n_tp], refs[n_tp:]
    dq_ref, refs = refs[0], refs[1:]
    dkv_refs, refs = refs[:n_chunk], refs[n_chunk:]
    qm_ref, gom_ref, dqt_ref, acck_ref, accv_ref, go_ref, mixed_ref = refs
    q_len, width = q_ref.shape
    ctx, tp = scalars[1], scalars[2]
    for o in range(n_tp):
        go_ref[lanes(tp, o, q_len // n_tp), :] = gm_refs[o][...]
        mixed_ref[lanes(tp, o, q_len // n_tp), :] = mixed_refs[o][...]
    deltas = []
    for start in range(0, q_len, tq):
        rows = slice(start, start + tq)
        prod = (go_ref[rows, :].astype(F32) * mixed_ref[rows, :].astype(F32)).T
        sums = [
            jnp.sum(prod[h * HD : (h + 1) * HD, :], axis=0, keepdims=True) for h in range(heads)
        ]
        deltas.append(sums)
    lane = lax.broadcasted_iota(jnp.int32, (tq, width), 1)
    nq = q_len // tq
    for qi in range(nq):
        rows = slice(qi * tq, (qi + 1) * tq)
        qv = q_ref[rows, :] * BF16(0.125)
        gv = go_ref[rows, :]
        for h in range(heads):
            mine = (lane >= h * HD) & (lane < (h + 1) * HD)
            qm_ref[h, rows, :] = jnp.where(mine, qv, jnp.zeros_like(qv))
            gom_ref[h, rows, :] = jnp.where(mine, gv, jnp.zeros_like(gv))
    dqt_ref[...] = jnp.zeros_like(dqt_ref)
    for c in range(n_chunk):
        kv = kv_refs[c]
        dkv = dkv_refs[c]
        cbase = (ctx ^ c) * q_len

        def step(ki, carry, kv=kv, dkv=dkv, cbase=cbase):
            kb = cbase + ki * tk
            krows = pl.ds(pl.multiple_of(ki * tk, tk), tk)
            live = [
                (kb <= ctx * q_len + (qi + 1) * tq - 1) & (kb + tk - 1 >= scalars[3 + qi])
                for qi in range(nq)
            ]
            some = functools.reduce(jnp.logical_or, live)

            @pl.when(jnp.logical_not(some))
            def _():
                dkv[krows, :] = jnp.zeros((tk, 2 * width), BF16)

            @pl.when(some)
            def _():
                acck_ref[...] = jnp.zeros_like(acck_ref)
                accv_ref[...] = jnp.zeros_like(accv_ref)
                k = kv[krows, 0:width]
                v = kv[krows, width : 2 * width]
                kt = k.T
                kpos = kb + lax.broadcasted_iota(jnp.int32, (tk, 1), 0)
                for qi in range(nq):

                    @pl.when(live[qi])
                    def _(qi=qi):
                        rows = slice(qi * tq, (qi + 1) * tq)
                        qpos = (
                            ctx * q_len + qi * tq + lax.broadcasted_iota(jnp.int32, (1, tq), 1)
                        )
                        ok = (kpos >= lo_ref[0:1, rows]) & (kpos <= qpos)
                        dk = acck_ref[...]
                        dv = accv_ref[...]
                        for h in range(heads):
                            qh = qm_ref[h, rows, :]
                            gh = gom_ref[h, rows, :]
                            s = dot(k, qh, 1, 1)
                            p = jnp.where(ok, jnp.exp(s - lse_ref[h : h + 1, rows]), 0.0)
                            dp = dot(v, gh, 1, 1)
                            ds = (p * (dp - deltas[qi][h])).astype(BF16)
                            dv = dv + dot(p.astype(BF16), gh, 1, 0)
                            dk = dk + dot(ds, qh, 1, 0)
                            hs = slice(h * HD, (h + 1) * HD)
                            dqt_ref[hs, rows] = dqt_ref[hs, rows] + dot(kt[hs, :], ds, 1, 0)
                        acck_ref[...] = dk
                        accv_ref[...] = dv

                dkv[krows, 0:width] = acck_ref[...].astype(BF16)
                dkv[krows, width : 2 * width] = accv_ref[...].astype(BF16)

            return carry

        lax.fori_loop(0, q_len // tk, step, 0)
    for qi in range(nq):
        rows = slice(qi * tq, (qi + 1) * tq)
        dq_ref[rows, :] = (dqt_ref[:, rows].T * 0.125).astype(BF16)


def normal(value):
    mean = jnp.mean(value, axis=-1, keepdims=True)
    centered = value - mean
    inv = lax.rsqrt(jnp.mean(centered * centered, axis=-1, keepdims=True) + 1e-05)
    return centered * inv, inv


def normal_back(grad_out, norm, inv, gain):
    grad = grad_out * gain
    centered = grad - jnp.mean(grad, axis=-1, keepdims=True)
    return inv * (centered - norm * jnp.mean(grad * norm, axis=-1, keepdims=True))


def merge_kernel(n_tp, rows_ref, wide_ref, *refs):
    mixed, refs = refs[:n_tp], refs[n_tp:]
    weights, (hidden_ref, normed_ref) = refs[:-2], refs[-2:]
    values = jnp.concatenate([ref[...] for ref in mixed], axis=1)
    block = weights[0].shape[0]
    for place, ref in enumerate(weights):
        cols = slice(place * block, (place + 1) * block)
        made = dot(values, ref[...], 1, 1)
        hidden_ref[:, cols] = rows_ref[:, cols].astype(F32) + made + wide_ref[2:3, cols]
    norm, _ = normal(hidden_ref[...])
    normed_ref[...] = (norm * wide_ref[3:4, :] + wide_ref[4:5, :]).astype(BF16)


def dense_kernel(count, expand_ref, *refs):
    normed, refs = refs[:count], refs[count:]
    grads, refs = refs[:count], refs[count:]
    weights, outs = refs[: -4 * count - 1], refs[-4 * count - 1 :]
    acts, pres, normed_outs, mlp_outs = (outs[i * count : (i + 1) * count] for i in range(4))
    sum_ref = outs[-1]
    block = weights[0].shape[0] // 2
    height = normed[0].shape[0]
    hidden = expand_ref.shape[1]
    step = min(hidden, 512)
    value = jnp.concatenate([ref[...] for ref in normed], axis=0)
    grad = jnp.concatenate([ref[...] for ref in grads], axis=0)
    back = forth = None
    for start in range(0, hidden, step):
        cols = slice(start, start + step)
        expand = jnp.concatenate([ref[:block, cols] for ref in weights], axis=0)
        shrink = jnp.concatenate([ref[block:, cols] for ref in weights], axis=0)
        pre = dot(value, expand, 1, 0) + expand_ref[:, cols]
        square = pre * pre
        inner = jnp.tanh(0.7978845608028654 * (pre + 0.044715 * square * pre))
        act = (0.5 * pre * (1.0 + inner)).astype(BF16)
        slope = 0.5 * (1.0 + inner) + (0.5 * 0.7978845608028654) * pre * (
            1.0 - inner * inner
        ) * (1.0 + (3.0 * 0.044715) * square)
        low = (dot(grad, shrink, 1, 0) * slope).astype(BF16)
        sum_ref[:, cols] = jnp.sum(low.astype(F32), axis=0, keepdims=True)
        for i in range(count):
            rows = slice(i * height, (i + 1) * height)
            acts[i][:, cols] = act[rows]
            pres[i][:, cols] = low[rows]
        more = dot(low, expand, 1, 1)
        also = dot(act, shrink, 1, 1)
        back = more if back is None else back + more
        forth = also if forth is None else forth + also
    for i in range(count):
        rows = slice(i * height, (i + 1) * height)
        normed_outs[i][...] = back[rows].astype(BF16)
        mlp_outs[i][...] = forth[rows].astype(BF16)


def hidden_back_kernel(n_tp, grad_ref, hidden_ref, wide_ref, *refs):
    parts, refs = refs[:n_tp], refs[n_tp:]
    weights, outs = refs[: -3 - n_tp], refs[-3 - n_tp :]
    back_ref, low_ref, sums_ref = outs[:3]
    total = total_of(parts)
    norm, inv = normal(hidden_ref[...])
    grad = grad_ref[...].astype(F32)
    back = grad + normal_back(total, norm, inv, wide_ref[3:4, :])
    back_ref[...] = back
    low = back.astype(BF16)
    low_ref[...] = low
    width = outs[3].shape[1]
    for o in range(n_tp):
        cols = slice(o * width, (o + 1) * width)
        weight = jnp.concatenate([ref[:, cols] for ref in weights], axis=0)
        outs[3 + o][...] = dot(low, weight, 1, 0).astype(BF16)
    sums_ref[...] = jnp.concatenate(
        [jnp.sum(v, axis=0, keepdims=True) for v in (back, total * norm, total, grad)], axis=0
    )


def outer_kernel(order, spans, scalars, *refs):
    out_ref = refs[-1]
    tall = out_ref.shape[1] // len(spans)
    base = 0
    for many, more in spans:
        left, refs = refs[:many], refs[many:]
        right, refs = refs[:more], refs[more:]
        a = jnp.concatenate([ref[...] for ref in left], axis=0)
        b = jnp.concatenate([ref[...] for ref in right], axis=0)
        for place, offset in enumerate(order):
            made = dot(a[:, place * tall : (place + 1) * tall], b, 0, 0).astype(BF16)
            out_ref[scalars[0] ^ offset, base : base + tall, :] = made
        base += tall


def last_outer_kernel(order, n_tp, scalars, normed_ref, query_ref, pair_ref, grad_ref, *refs):
    mixed, out_ref = refs[:n_tp], refs[n_tp]
    tall = out_ref.shape[1]
    width = query_ref.shape[1]
    values = jnp.concatenate([ref[...] for ref in mixed], axis=1)
    for place, offset in enumerate(order):
        rows = slice(place * tall, (place + 1) * tall)
        target = scalars[0] ^ offset
        left = normed_ref[:, rows]
        out_ref[target, :, :width] = dot(left, query_ref[...], 0, 0).astype(BF16)
        out_ref[target, :, width : 3 * width] = dot(left, pair_ref[...], 0, 0).astype(BF16)
        out_ref[target, :, 3 * width :] = dot(grad_ref[:, rows], values, 0, 0).astype(BF16)


def join_kernel(left_ref, right_ref, out_ref):
    total = left_ref[...].astype(F32) + right_ref[...].astype(F32)
    out_ref[...] = total.astype(out_ref.dtype)


def sum_of(ref):
    total = ref[0].astype(F32)
    for i in range(1, ref.shape[0]):
        total = total + ref[i].astype(F32)
    return total


def dense_total_kernel(in_ref, expand_ref, shrink_ref):
    block = expand_ref.shape[0]
    expand_ref[...] = in_ref[:block, :].astype(F32)
    shrink_ref[...] = in_ref[block:, :].astype(F32).T


def last_total_kernel(in_ref, attend_ref, *outs):
    parts, _, width = attend_ref.shape
    for c in range(parts):
        attend_ref[c] = in_ref[:, c * width : (c + 1) * width].astype(F32)
    for o, ref in enumerate(outs):
        ref[...] = in_ref[:, (parts + o) * width : (parts + o + 1) * width]


def merge_turned_kernel(*refs):
    refs[-1][...] = total_of(refs[:-1]).T


def total_of(refs):
    total = refs[0][...].astype(F32)
    for ref in refs[1:]:
        total = total + ref[...].astype(F32)
    return total


def layer_kernel(order, scalars, hidden_ref, wide_ref, *refs):
    total = total_of(refs[:-1])
    out_ref = refs[-1]
    value = (hidden_ref[...] + total + wide_ref[5:6, :]).astype(BF16)
    size = value.shape[1] // len(order)
    for place, offset in enumerate(order):
        out_ref[:, lanes(scalars[0], offset, size)] = value[:, place * size : (place + 1) * size]


def input_kernel(order, scalars, rows_ref, back_ref, wide_ref, *refs):
    out_ref, sums_ref = refs[-2:]
    total = total_of(refs[:-2])
    norm, inv = normal(rows_ref[...].astype(F32))
    value = (back_ref[...] + normal_back(total, norm, inv, wide_ref[0:1, :])).astype(BF16)
    size = value.shape[1] // len(order)
    for place, offset in enumerate(order):
        out_ref[:, lanes(scalars[0], offset, size)] = value[:, place * size : (place + 1) * size]
    sums_ref[...] = jnp.concatenate(
        [jnp.sum(v, axis=0, keepdims=True) for v in (total * norm, total)], axis=0
    )


def place_kernel(count, scalars, *refs):
    height = refs[0].shape[0]
    for o in range(count):
        start = pl.multiple_of((scalars[2] ^ o) * height, height)
        refs[count][pl.ds(start, height), :] = refs[o][...]


def project_back_kernel(block, n_pair, n_tp, scalars, dq_ref, *refs):
    many = len(refs) - n_tp - 2
    outs = refs[many:]
    pair_ref, sums_ref = outs[n_tp:]
    pair = total_of(refs[:n_pair]).astype(BF16)
    weights = refs[n_pair:many]
    pair_ref[...] = pair
    width = dq_ref.shape[1]
    weight = rows_of(weights, 0, block)
    height = outs[0].shape[0]
    for o in range(n_tp):
        rows = pl.ds(pl.multiple_of((scalars[2] ^ o) * height, height), height)
        both = jnp.concatenate([dq_ref[rows, :], pair_ref[rows, :]], axis=1)
        outs[o][...] = dot(both, weight, 1, 1).astype(BF16)
    sums_ref[...] = jnp.concatenate(
        [
            jnp.sum(v, axis=0, keepdims=True)
            for v in (dq_ref[...].astype(F32), pair[:, width:].astype(F32))
        ],
        axis=0,
    )


def small_kernel(order, head_block, n_tp, scalars, two_ref, four_ref, attend_ref, *refs):
    index = scalars[0]
    out_ref = refs[-1]
    hidden = total_of(refs[:-1])
    size = out_ref.shape[2]
    attend = jnp.concatenate([attend_ref[...], jnp.zeros((6, attend_ref.shape[1]), F32)], axis=0)
    for place, offset in enumerate(order):
        cols = slice(place * size, (place + 1) * size)
        block = index ^ offset
        turned = pltpu.roll(attend, attend.shape[1] - block * head_block, 1)
        last = jnp.concatenate(
            [
                turned[0:1, :head_block],
                turned[1:2, :head_block],
                jnp.zeros((1, size - 2 * head_block), F32),
            ],
            axis=1,
        )
        mine = jnp.zeros((1, size), F32)
        for j in range(len(order)):
            mine = mine + jnp.where(block == j, hidden[:, j * size : (j + 1) * size], 0.0)
        made = jnp.concatenate([two_ref[:, cols], four_ref[:, cols], mine, last], axis=0)
        for o in range(n_tp):
            out_ref[block * n_tp + o] = made


def small_total_kernel(n_tp, scalars, in_ref, *outs):
    total = sum_of(in_ref)
    local = in_ref[scalars[2]]
    for i in range(1, in_ref.shape[0] // n_tp):
        local = local + in_ref[i * n_tp + scalars[2]]
    for i in range(6):
        outs[i][...] = total[i : i + 1, :]
    outs[6][...] = local[6:7, :]
    size = outs[7].shape[1]
    outs[7][...] = jnp.concatenate([local[7:8, :size], local[7:8, size : 2 * size]], axis=0)


def after(value, *others):
    return lax.optimization_barrier((value, *others))[0]


def body(
    sizes,
    layer_input,
    cotangent,
    segment_ids,
    norm1_gain,
    norm1_bias,
    attend_weight,
    attend_bias,
    merge_weight,
    merge_bias,
    norm2_gain,
    norm2_bias,
    expand_weight,
    expand_bias,
    shrink_weight,
    shrink_bias,
):
    n_dp, n_ctx, n_tp = sizes
    group = n_dp * n_ctx
    seqs, q_len, wide = layer_input.shape
    assert seqs == 1
    block = wide // group
    width = attend_weight.shape[2]
    heads = width // HD
    hidden_width = expand_weight.shape[1]
    height = q_len // n_tp
    bias_block = expand_bias.shape[0]
    head_block = attend_bias.shape[1]
    tile = min(256, q_len)
    direct = (n_dp, n_ctx) == (2, 4) and block % 128 == 0
    direct = direct and bias_block == block and 2 * head_block <= block
    order = [0, 2, 4, 6, 1, 3, 5, 7] if direct else [0]
    ctx = lax.axis_index("ctx")
    tp = lax.axis_index("tp")
    me = lax.axis_index("dp") * n_ctx + ctx if direct else 0 * ctx
    plane = ("dp", "ctx")

    def plane_swap(value, offset):
        return lax.ppermute(value, plane, [(i, i ^ offset) for i in range(group)])

    def ctx_swap(value, offset):
        return lax.ppermute(value, "ctx", [(i, i ^ offset) for i in range(n_ctx)])

    def tp_swap(value, offset):
        return lax.ppermute(value, "tp", [(i, i ^ offset) for i in range(n_tp)])

    def with_cores(even):
        return even + [ctx_swap(v, 1) for v in even]

    def tp_gather(value):
        return [value] + [tp_swap(value, o) for o in range(1, n_tp)]

    def tp_exchange(parts):
        return [parts[0]] + [tp_swap(parts[o], o) for o in range(1, n_tp)]

    smalls = (
        norm1_gain,
        norm1_bias,
        merge_bias,
        norm2_gain,
        norm2_bias,
        shrink_bias,
        expand_bias,
    )
    if direct:
        (pack,) = call(
            pack_kernel,
            "pack",
            None,
            [jnp.swapaxes(attend_weight, 0, 1)]
            + [jnp.reshape(v, (1, block)) for v in smalls]
            + [attend_bias],
            [shape((block + 8, 3 * width), BF16)],
        )
        first_x = plane_swap(pack, 2)
        first_y = plane_swap(pack, 4)
        merge_rows = tp_gather(after(merge_weight, pack))
        (rest,) = call(
            turn_kernel,
            "turn",
            None,
            [expand_weight, shrink_weight, *merge_rows],
            [shape((3 * block, wide), BF16)],
        )
        first_xy = plane_swap(first_x, 4)
        first = with_cores([pack, first_x, first_y, first_xy])
        rest_x = plane_swap(after(rest, first_x), 2)
        rest_y = plane_swap(after(rest, first_xy), 4)
        rest_xy = plane_swap(rest_x, 4)
        given = []
    else:

        def whole(value, axis):
            return lax.all_gather(value, plane, axis=axis, tiled=True)

        first = [jnp.reshape(whole(attend_weight, 0), (wide, 3 * width))]
        merge_rows = whole(jnp.concatenate(tp_gather(merge_weight.T), axis=1), 0)
        rest_all = [
            jnp.concatenate([whole(expand_weight, 0), whole(shrink_weight.T, 0), merge_rows], 0)
        ]
        wide_rows = whole(jnp.stack(smalls[:6]), 1).astype(F32)
        given = [
            jnp.pad(wide_rows, ((0, 2), (0, 0))),
            whole(expand_bias, 0).astype(F32)[None],
            whole(attend_bias, 1).astype(F32),
        ]
    span = block if direct else wide

    seg_all = segment_ids[0]
    seg_query = lax.dynamic_slice_in_dim(seg_all, ctx * q_len, q_len, 0)
    lows = jnp.sum(
        (seg_all[:, None] < seg_query[None, :]).astype(jnp.int32), axis=0, keepdims=True
    )
    place = jnp.stack([me, ctx, tp]).astype(jnp.int32)
    limits = jnp.concatenate([place, lows[0, ::tile]], axis=0)
    keep = jnp.broadcast_to((seg_query > 0).astype(BF16)[:, None], (q_len, 128))

    normed1, query, pair, input_rows, wide_rows, expand_add, attend_add = call(
        functools.partial(project_kernel, order, span, head_block),
        "project",
        place,
        [layer_input[0], *first, *given],
        [
            shape((q_len, wide), BF16),
            shape((q_len, width), BF16),
            shape((q_len, 2 * width), BF16),
            shape((height, wide), BF16),
            shape((8, wide), F32),
            shape((1, hidden_width), F32),
            shape((2, width), F32),
        ],
        flops=6 * q_len * wide * width,
    )
    near = [pair] + [ctx_swap(pair, o) for o in range(2, n_ctx, 2)]
    pairs = []
    for value in near:
        pairs += [value, ctx_swap(value, 1)]
    grad_rows = call(
        functools.partial(grad_order_kernel, order, n_tp),
        "order_grad",
        place,
        [after(cotangent[0], pair), keep],
        [shape((height, wide), BF16)] * n_tp,
    )
    pairs[-1] = after(pairs[-1], grad_rows[0], limits)
    out = call(
        functools.partial(attend_kernel, heads, tile, tile, n_ctx, n_tp),
        "attention",
        limits,
        [lows, query, *pairs],
        [shape((height, width), BF16)] * n_tp + [shape((heads, q_len), F32)],
        [
            pltpu.VMEM((heads, tile, width), BF16),
            pltpu.VMEM((width, tile), F32),
            pltpu.VMEM((8, tile), F32),
            pltpu.VMEM((8, tile), F32),
            pltpu.VMEM((q_len, width), BF16),
        ],
        flops=4 * q_len * q_len * n_ctx * width,
    )
    mixed, lse = out[:n_tp], out[n_tp]
    if direct:
        rest_all = with_cores([after(v, mixed[0]) for v in (rest, rest_x, rest_y, rest_xy)])
    merge_all = [(v, (span, wide), (2, 0)) for v in rest_all]
    dense_all = [(v, (2 * span, wide), (0, 0)) for v in rest_all]
    mixed_rows = tp_exchange(mixed)
    hidden, normed2 = call(
        functools.partial(merge_kernel, n_tp),
        "merge",
        None,
        [input_rows, wide_rows, *mixed_rows, *merge_all],
        [shape((height, wide), F32), shape((height, wide), BF16)],
        flops=2 * height * wide * wide,
    )

    normed_all = tp_gather(normed2)
    picks = [[o for o in range(n_tp) if o % 4 in (0, 2)], [o for o in range(n_tp) if o % 4 in (1, 3)]]
    acts, pres, parts, mlps = ([None] * n_tp for _ in range(4))
    sums = []
    for pick in picks:
        count = len(pick)
        if sums:
            normed_all[3] = after(normed_all[3], sums[0])
        out = call(
            functools.partial(dense_kernel, count),
            "dense",
            None,
            [expand_add]
            + [normed_all[o] for o in pick]
            + [grad_rows[o] for o in pick]
            + dense_all,
            [shape((height, hidden_width), BF16)] * (2 * count)
            + [shape((height, wide), BF16)] * (2 * count)
            + [shape((1, hidden_width), F32)],
            flops=8 * count * height * wide * hidden_width,
        )
        for i, o in enumerate(pick):
            acts[o], pres[o], parts[o], mlps[o] = (out[j * count + i] for j in range(4))
        sums.append(out[-1])
    grad_parts = tp_exchange(parts)
    if direct:
        (dense_outer,) = call(
            functools.partial(outer_kernel, order, [(n_tp, n_tp)] * 2),
            "dense_outer",
            place,
            [*normed_all, *pres, *grad_rows, *acts],
            [shape((group, 2 * block, hidden_width), BF16)],
            flops=4 * wide * hidden_width * q_len,
        )
        grad_parts[-1] = after(grad_parts[-1], dense_outer)
    out = call(
        functools.partial(hidden_back_kernel, n_tp),
        "hidden_back",
        None,
        [grad_rows[0], hidden, wide_rows, *grad_parts, *merge_all],
        [
            shape((height, wide), F32),
            shape((height, wide), BF16),
            shape((4, wide), F32),
        ]
        + [shape((height, width), BF16)] * n_tp,
        flops=2 * height * wide * wide,
    )
    hidden_grad, grad_attn, four, grad_mixed = out[0], out[1], out[2], tp_exchange(out[3:])
    mlps = tp_exchange([mlps[0]] + [after(v, grad_mixed[1]) for v in mlps[1:]])

    out = call(
        functools.partial(attend_back_kernel, heads, tile, tile, n_ctx, n_tp),
        "attention_back",
        limits,
        [lows, lse, query, *pairs, *mixed, *grad_mixed],
        [shape((q_len, width), BF16)] + [shape((q_len, 2 * width), BF16)] * n_ctx,
        [
            pltpu.VMEM((heads, q_len, width), BF16),
            pltpu.VMEM((heads, q_len, width), BF16),
            pltpu.VMEM((width, q_len), F32),
            pltpu.VMEM((tile, width), F32),
            pltpu.VMEM((tile, width), F32),
            pltpu.VMEM((q_len, width), BF16),
            pltpu.VMEM((q_len, width), BF16),
        ],
        flops=10 * q_len * q_len * n_ctx * width,
    )
    grad_query, grad_pairs = out[0], out[1:]
    joined = []
    for o in reversed(range(0, n_ctx, 2)):
        other = ctx_swap(grad_pairs[o + 1], 1)
        if joined:
            other = after(other, joined[-1])
        (total,) = call(
            join_kernel, "join", None, [other, grad_pairs[o]], [shape(other.shape, BF16)]
        )
        joined.append(total)
    joined = joined[::-1]
    (layer_part,) = call(
        functools.partial(layer_kernel, order),
        "layer",
        place,
        [after(hidden, joined[-1]), wide_rows, *mlps],
        [shape((height, wide), BF16)],
    )
    joined = [joined[0]] + [ctx_swap(v, 2 * i) for i, v in enumerate(joined) if i]
    joined[-1] = after(joined[-1], layer_part)
    out = call(
        functools.partial(project_back_kernel, span, len(joined), n_tp),
        "project_back",
        place,
        [grad_query, *joined, *first],
        [shape((height, wide), BF16)] * n_tp
        + [shape((q_len, 2 * width), BF16), shape((2, width), F32)],
        flops=6 * q_len * wide * width,
    )
    normed1_parts, grad_pair, attend_sums = tp_exchange(out[:n_tp]), out[n_tp], out[n_tp + 1]
    layer_parts = tp_gather(after(layer_part, normed1_parts[1]))
    if direct:
        dense_part = lax.psum_scatter(
            jnp.reshape(after(dense_outer, hidden_grad), (2 * wide, hidden_width)),
            plane,
            scatter_dimension=0,
            tiled=True,
        )
        (last_outer,) = call(
            functools.partial(last_outer_kernel, order, n_tp),
            "last_outer",
            place,
            [normed1, grad_query, grad_pair, grad_attn, *mixed_rows],
            [shape((group, block, 3 * width + wide), BF16)],
            flops=6 * wide * width * q_len + 2 * height * wide * wide,
        )
        last_part = lax.psum_scatter(
            jnp.reshape(last_outer, (wide, 3 * width + wide)),
            plane,
            scatter_dimension=0,
            tiled=True,
        )
        grad_expand, grad_shrink = call(
            dense_total_kernel,
            "dense_total",
            None,
            [after(dense_part, grad_pair)],
            [shape((block, hidden_width), F32), shape((hidden_width, block), F32)],
        )
        normed1_parts[-1] = after(normed1_parts[-1], last_outer, grad_expand)
    input_part, two = call(
        functools.partial(input_kernel, order),
        "input_back",
        place,
        [input_rows, hidden_grad, wide_rows, *normed1_parts],
        [shape((height, wide), BF16), shape((2, wide), F32)],
    )
    input_parts = tp_gather(input_part)

    def placed(parts):
        (result,) = call(
            functools.partial(place_kernel, n_tp),
            "place",
            place,
            parts,
            [shape((q_len, wide), BF16)],
        )
        return result

    layer_output = placed(layer_parts)

    if direct:
        out = call(
            last_total_kernel,
            "last_total",
            None,
            [last_part],
            [shape((3, block, width), F32)] + [shape((block, width), BF16)] * n_tp,
        )
        grad_attend = out[0]
        (grad_merge,) = call(
            merge_turned_kernel,
            "merge_turned",
            None,
            tp_exchange(out[1:]),
            [shape((width, block), F32)],
        )
        (small,) = call(
            functools.partial(small_kernel, order, head_block, n_tp),
            "small",
            place,
            [two, four, attend_sums, *sums],
            [shape((group * n_tp, 8, block), F32)],
        )
        table = call(
            functools.partial(small_total_kernel, n_tp),
            "small_total",
            place,
            [lax.all_to_all(small, ("dp", "ctx", "tp"), 0, 0)],
            [shape((1, block), F32)] * 7 + [shape((2, head_block), F32)],
        )
        rows = [jnp.reshape(v, (block,)) for v in table[:7]]
        expand_sum, attend_sum = rows[6], table[7]
        input_parts[-1] = after(input_parts[-1], layer_output, *table)
        grad_attend = jnp.swapaxes(grad_attend, 0, 1)
    else:

        def cut(value, axis):
            return lax.psum_scatter(value, plane, scatter_dimension=axis, tiled=True)

        def outer_of(left, right):
            return cut(
                dot(jnp.concatenate(left), jnp.concatenate(right), 0, 0).astype(BF16), 0
            ).astype(F32)

        grad_expand = outer_of(normed_all, pres)
        grad_shrink = outer_of(grad_rows, acts).T
        grad_merge = outer_of([grad_attn], [jnp.concatenate(mixed_rows, axis=1)]).astype(BF16)
        grad_merge = [grad_merge[:, o * width : (o + 1) * width] for o in range(n_tp)]
        grad_merge = sum(v.astype(F32) for v in tp_exchange(grad_merge)).T
        grad_attend = outer_of([normed1], [jnp.concatenate([grad_query, grad_pair], axis=1)])
        grad_attend = jnp.reshape(grad_attend, (block, 3, width))
        table = lax.psum(cut(jnp.concatenate([two, four], axis=0), 1), "tp")
        rows = [table[i] for i in range(6)]
        expand_sum = cut(sum(sums)[0], 0)
        attend_sum = cut(attend_sums, 1)
    input_grad = placed(input_parts)
    return (
        layer_output[None],
        input_grad[None],
        rows[0],
        rows[1],
        grad_attend,
        attend_sum,
        grad_merge,
        rows[2],
        rows[3],
        rows[4],
        grad_expand,
        expand_sum,
        grad_shrink,
        rows[5],
    )


def solution(mesh):
    sizes = (mesh.shape["dp"], mesh.shape["ctx"], mesh.shape["tp"])
    return jax.shard_map(
        functools.partial(body, sizes),
        mesh=mesh,
        in_specs=(
            P("dp", "ctx", None),
            P("dp", "ctx", None),
            P("dp", None),
            P(("dp", "ctx")),
            P(("dp", "ctx")),
            P(("dp", "ctx"), None, "tp"),
            P(None, ("tp", "dp", "ctx")),
            P("tp", ("dp", "ctx")),
            P(("dp", "ctx")),
            P(("dp", "ctx")),
            P(("dp", "ctx")),
            P(("dp", "ctx"), "tp"),
            P(("tp", "dp", "ctx")),
            P("tp", ("dp", "ctx")),
            P(("dp", "ctx")),
        ),
        out_specs=(
            P("dp", "ctx", None),
            P("dp", "ctx", None),
            P(("dp", "ctx")),
            P(("dp", "ctx")),
            P(("dp", "ctx"), None, "tp"),
            P(None, ("tp", "dp", "ctx")),
            P("tp", ("dp", "ctx")),
            P(("dp", "ctx")),
            P(("dp", "ctx")),
            P(("dp", "ctx")),
            P(("dp", "ctx"), "tp"),
            P(("tp", "dp", "ctx")),
            P("tp", ("dp", "ctx")),
            P(("dp", "ctx")),
        ),
        check_vma=False,
    )
```

time: 684 us -> 332 us (0.49)
  waiting for transfers between devices: 406 us -> 133 us
  blocking collectives: 104 us -> 0 us
  matrix products: 86.7 us -> 0 us
  Pallas kernels: 0 us -> 83.9 us
  starting transfers between devices: 1.25 us -> 82.8 us
  other arithmetic: 38.4 us -> 1.75 us
  local copies, waits for them, and re-layouts: 24.8 us -> 14.8 us
    reduce_scatter x6 -> x2, waiting for transfers between devices: 181 us -> 0.02 us  [the longest x1 0.02 us: body(): lax.psum_scatter(jnp.reshape(last_outer, (wide, 3 * width + wide)), plane...]
    psum x3 -> x0, waiting for transfers between devices: 158 us -> none  [the longest x1 88.9 us: body(): mlp_out = lax.psum(mlp_part.astype(jnp.bfloat16), 'tp').astype(jnp.float32)]
    ppermute x0 -> x50, waiting for transfers between devices: none -> 124 us  [the longest x30 95.9 us: tp_swap(): return lax.ppermute(value, 'tp', [(i, i ^ offset) for i in range(n_tp)])]
    dot_general x36 -> x0, matrix products: 86.7 us -> none  [the longest x4 15.5 us: body(): jnp.einsum('sqd,skd->sqk', grad_out_h, value_per_head, preferred_element_...]
    pallas_call x0 -> x24, Pallas kernels: none -> 83.9 us  [call(): pl.pallas_call(kernel, grid=(1,), out_shape=tuple(outs), in_specs=[pl.Blo...]
    ppermute x0 -> x50, starting transfers between devices: none -> 80.2 us  [the longest x30 50.7 us: tp_swap(): return lax.ppermute(value, 'tp', [(i, i ^ offset) for i in range(n_tp)])]
    all_gather x9 -> x0, blocking collectives: 79.6 us -> none  [the longest x1 10.3 us: body(): lax.all_gather(norm1_gain, ('dp', 'ctx'), axis=0, tiled=True)]
    all_gather x5 -> x0, waiting for transfers between devices: 65.1 us -> none  [the longest x1 26.9 us: body(): lax.all_gather(expand_weight, ('dp', 'ctx'), axis=0, tiled=True)]
  transfers between devices with their start and end apart: 15 -> 53, of which waited for: 13 -> 25; matrix products, arithmetic and copies ran while one was open for 14% -> 1% of each run, Pallas kernels for 0% -> 20%
where the time goes in v1:
time: 332 us; the launch traced here: 331 us
  waiting for transfers between devices  133 us (40%)
  Pallas kernels  83.9 us (25%)
  starting transfers between devices  82.8 us (25%)
  local copies, waits for them, and re-layouts  14.8 us (4%)
  between operations  14.5 us (4%)
    ppermute x30, waiting for transfers between devices, tp_swap(): return lax.ppermute(value, 'tp', [(i, i ^ offset) for i in range(n_tp)])  95.9 us
    pallas_call x24, Pallas kernels, call(): pl.pallas_call(kernel, grid=(1,), out_shape=tuple(outs), in_specs=[pl.Blo...  83.9 us
    ppermute x30, starting transfers between devices, tp_swap(): return lax.ppermute(value, 'tp', [(i, i ^ offset) for i in range(n_tp)])  50.7 us
    ppermute x14, starting transfers between devices, ctx_swap(): return lax.ppermute(value, 'ctx', [(i, i ^ offset) for i in range(n_ctx)])  20.7 us
    ppermute x6, waiting for transfers between devices, plane_swap(): return lax.ppermute(value, plane, [(i, i ^ offset) for i in range(group)])  16.8 us
    unnamed x124, local copies, waits for them, and re-layouts  14 us
    ppermute x14, waiting for transfers between devices, ctx_swap(): return lax.ppermute(value, 'ctx', [(i, i ^ offset) for i in range(n_ctx)])  10.9 us
    all_to_all x1, waiting for transfers between devices, body(): lax.all_to_all(small, ('dp', 'ctx', 'tp'), 0, 0)  9.41 us
  transfers between devices with their start and end apart: 53, of which 25 were waited for; matrix products, arithmetic and copies ran while one was open for 1% of the time, Pallas kernels for 20%

profile of v1, /device:TPU:0, one launch (start us, length us, event | category | flops | bytes accessed | tf_op | source)
XLA Modules:
  0.0 330.8 jit_solution(14698538792170133925)
XLA Ops:
  9.0 2.9 collective-permute-start
  13.5 3.9 %collective-permute-done.refs_1_.refs_3_ = bf16[136,768]{1,0:T(8,128)(2,1)S(1)} collective-permute-done((bf16[136,768]{1,0:T(8,128)(2,1)}, bf16[136,768]{1,0:T(8,128)(2,1)S(1)}, u32[]{:S(2)}, u32[]{:S(2)}) %collective-permute-start) | collective-permute-done | bytes 208928 | tf_op jit(solution)/shard_map/ppermute | solution.py:593
  19.1 3.6 %collective-permute-start.15 = (bf16[256,128]{1,0:T(8,128)(2,1)}, bf16[256,128]{1,0:T(8,128)(2,1)S(1)}, u32[]{:S(2)}, u32[]{:S(2)}) collective-permute-start(bf16[256,128]{1,0:T(8,128)(2,1)} %refs_0_), channel_id=1, source_target_pairs={{0,3},{1,2},{2,1},{3,0},{4,7},{5,6},{6,5},{7,4},{8,11},{9,10},{10,... | collective-permute-start | bytes 196616 | tf_op jit(solution)/shard_map/ppermute | solution.py:599
  36.0 4.6 %project.1 = (bf16[512,1024]{1,0:T(8,128)(2,1)}, bf16[512,256]{1,0:T(8,128)(2,1)}, bf16[512,512]{1,0:T(8,128)(2,1)}, bf16[128,1024]{1,0:T(8,128)(2,1)}, f32[8,10...) custom-call(s32[3]{0:T(128)} %pad_add_fusion.scalars, bf16[512,1024]{1,0:T(8,128)(2,1)} %bitcast.49, ...), custom_call_target="tpu_custom_call" | custom-call | flops 805306368 | bytes 4855808 | tf_op jit(solution)/shard_map/project/pallas_call | solution.py:39
  41.6 10.5 %collective-permute-done.16.refs_5_ = bf16[384,1024]{1,0:T(8,128)(2,1)S(1)} collective-permute-done((bf16[384,1024]{1,0:T(8,128)(2,1)}, bf16[384,1024]{1,0:T(8,128)(2,1)S(1)}, u32[]{:S(2)}, u32[]{:S(2)}) %collective-permute-start.16) | collective-permute-done | bytes 786464 | tf_op jit(solution)/shard_map/ppermute | solution.py:593
  52.7 8.4 %collective-permute-done.8.refs_2_ = bf16[512,512]{1,0:T(8,128)(2,1)} collective-permute-done((bf16[512,512]{1,0:T(8,128)(2,1)}, bf16[512,512]{1,0:T(8,128)(2,1)}, u32[]{:S(2)}, u32[]{:S(2)}) %collective-permute-start.8) | collective-permute-done | bytes 524320 | tf_op jit(solution)/shard_map/ppermute | solution.py:596
  65.7 6.1 %attention.1 = (bf16[128,256]{1,0:T(8,128)(2,1)}, bf16[128,256]{1,0:T(8,128)(2,1)}, bf16[128,256]{1,0:T(8,128)(2,1)}, bf16[128,256]{1,0:T(8,128)(2,1)}, f32[4,512]{1,0:T(4,128)}) custom-call(s32[5]{0:T(128)} %pad_add_fusion.1.scalars, s32[1,512]{1,0:T(1,128)} %bitcast.39, bf16[512,256]{1,0:T(8,128)(2,1)} %get-tuple-element.108.q_ref, ...), custom_call_target="tpu_custom_call" | custom-call | flops 1073741824 | bytes 2631680 | tf_op jit(solution)/shard_map/attention/pallas_call | solution.py:39
  71.9 2.8 collective-permute-start.19
  77.6 4.7 %collective-permute-done.10.refs_1_ = bf16[128,256]{1,0:T(8,128)(2,1)S(1)} collective-permute-done((bf16[128,256]{1,0:T(8,128)(2,1)}, bf16[128,256]{1,0:T(8,128)(2,1)S(1)}, u32[]{:S(2)}, u32[]{:S(2)}) %collective-permute-start.10) | collective-permute-done | bytes 65568 | tf_op jit(solution)/shard_map/ppermute | solution.py:599
  83.7 4.8 %collective-permute-done.11.refs_2_ = bf16[128,256]{1,0:T(8,128)(2,1)S(1)} collective-permute-done((bf16[128,256]{1,0:T(8,128)(2,1)}, bf16[128,256]{1,0:T(8,128)(2,1)S(1)}, u32[]{:S(2)}, u32[]{:S(2)}) %collective-permute-start.11) | collective-permute-done | bytes 65568 | tf_op jit(solution)/shard_map/ppermute | solution.py:599
  90.6 4.1 %collective-permute-done.12.refs_3_ = bf16[128,256]{1,0:T(8,128)(2,1)S(1)} collective-permute-done((bf16[128,256]{1,0:T(8,128)(2,1)}, bf16[128,256]{1,0:T(8,128)(2,1)S(1)}, u32[]{:S(2)}, u32[]{:S(2)}) %collective-permute-start.12) | collective-permute-done | bytes 65568 | tf_op jit(solution)/shard_map/ppermute | solution.py:599
  96.5 3.4 %merge.1 = (f32[128,1024]{1,0:T(8,128)}, bf16[128,1024]{1,0:T(8,128)(2,1)}) custom-call(bf16[128,1024]{1,0:T(8,128)(2,1)} %get-tuple-element.106.rows_ref, f32[8,1024]{1,0:T(8,128)} %get-tuple-element.107.wide_ref, bf16[128,256]{1,0:T(8,128)(2,1)} %get-tuple-element.113.refs_0_.refs_4_, bf16[128,256]{1,0:T(8,128)(2,1)} %copy-done.25, ...), custom_call_target="tpu_custom_call" | custom-call | flops 268435456 | bytes 3440640 | tf_op jit(solution)/shard_map/merge/pallas_call | solution.py:39
  103.3 15.1 %collective-permute-done.23.refs_1_.refs_2_ = bf16[128,1024]{1,0:T(8,128)(2,1)S(1)} collective-permute-done((bf16[128,1024]{1,0:T(8,128)(2,1)}, bf16[128,1024]{1,0:T(8,128)(2,1)S(1)}, u32[]{:S(2)}, u32[]{:S(2)}) %collective-permute-start.23) | collective-permute-done | bytes 262176 | tf_op jit(solution)/shard_map/ppermute | solution.py:599
  119.2 6.0 %dense.2 = (bf16[128,1024]{1,0:T(8,128)(2,1)}, bf16[128,1024]{1,0:T(8,128)(2,1)}, bf16[128,1024]{1,0:T(8,128)(2,1)}, bf16[128,1024]{1,0:T(8,128)(2,1)}, bf16[128...) custom-call(f32[1,1024]{1,0:T(1,128)} %get-tuple-element.126.expand_, ...), custom_call_target="tpu_custom_call" | custom-call | flops 2147483648 | bytes 7348224 | tf_op jit(solution)/shard_map/dense/pallas_call | solution.py:39
  126.0 6.0 %dense.3 = (bf16[128,1024]{1,0:T(8,128)(2,1)}, bf16[128,1024]{1,0:T(8,128)(2,1)}, bf16[128,1024]{1,0:T(8,128)(2,1)}, bf16[128,1024]{1,0:T(8,128)(2,1)}, bf16[128...) custom-call(f32[1,1024]{1,0:T(1,128)} %get-tuple-element.126.expand_, ...), custom_call_target="tpu_custom_call" | custom-call | flops 2147483648 | bytes 7348224 | tf_op jit(solution)/shard_map/dense/pallas_call | solution.py:39
  136.4 6.6 %dense_outer.1 = bf16[8,256,1024]{2,1,0:T(8,128)(2,1)} custom-call(s32[3]{0:T(128)} %pad_add_fusion.scalars, bf16[128,1024]{1,0:T(8,128)(2,1)} %get-tuple-element.127.refs_0_, bf16[128,1024]{1,0:T(8,128)(2,1)} %copy-done.23, bf16[128,1024]{1,0:T(8,128)(2,1)} %copy-done.19, bf16[128,1024]{1,0:T(8,128)(2,1)} %copy-done.21, ...), custom_call_target="tpu_custom_call" | custom-call | flops 2147483648 | bytes 8388608 | tf_op jit(solution)/shard_map/dense_outer/pallas_call | solution.py:39
  143.3 12.8 %collective-permute-done.27.refs_2_ = bf16[128,1024]{1,0:T(8,128)(2,1)S(1)} collective-permute-done((bf16[128,1024]{1,0:T(8,128)(2,1)S(1)}, bf16[128,1024]{1,0:T(8,128)(2,1)S(1)}, u32[]{:S(2)}, u32[]{:S(2)}) %collective-permute-start.27) | collective-permute-done | bytes 262176 | tf_op jit(solution)/shard_map/ppermute | solution.py:599
  156.9 3.8 %hidden_back.1 = (f32[128,1024]{1,0:T(8,128)}, bf16[128,1024]{1,0:T(8,128)(2,1)}, f32[4,1024]{1,0:T(4,128)}, bf16[128,256]{1,0:T(8,128)(2,1)}, bf16[128,256]{1,0...) custom-call(bf16[128,1024]{1,0:T(8,128)(2,1)} %get-tuple-element.111.refs_2_.refs_8_.grad_ref, ...), custom_call_target="tpu_custom_call" | custom-call | flops 268435456 | bytes 5029888 | tf_op jit(solution)/shard_map/hidden_back/pallas_call | solution.py:39
  167.1 3.0 collective-permute-done.31.refs_11_
  170.7 8.3 %attention_back.1 = (bf16[512,256]{1,0:T(8,128)(2,1)}, bf16[512,512]{1,0:T(8,128)(2,1)}, bf16[512,512]{1,0:T(8,128)(2,1)}, bf16[512,512]{1,0:T(8,128)(2,1)}, bf16[512,512]{1,0:T(8,128)(2,1)}) custom-call(s32[5]{0:T(128)} %pad_add_fusion.1.scalars, s32[1,512]{1,0:T(1,128)} %bitcast.40, f32[4,512]{1,0:T(4,128)} %get-tuple-element.125.lse_ref, ...), custom_call_target="tpu_custom_call" | custom-call | flops 2684354560 | bytes 5253120 | tf_op jit(solution)/shard_map/attention_back/pallas_call | solution.py:39
  184.2 15.3 %collective-permute-start.37 = (bf16[512,512]{1,0:T(8,128)(2,1)}, bf16[512,512]{1,0:T(8,128)(2,1)S(1)}, u32[]{:S(2)}, u32[]{:S(2)}) collective-permute-start(bf16[512,512]{1,0:T(8,128)(2,1)} %join.2), channel_id=1, source_target_pairs={{0,8},{4,12},{8,0},{12,4},{1,9},{5,13},{9,1},{13,5},{2,10},{6,14},... | collective-permute-start | bytes 1572872 | tf_op jit(solution)/shard_map/ppermute | solution.py:596
  206.8 5.4 %collective-permute-done.33.refs_1_ = bf16[128,1024]{1,0:T(8,128)(2,1)S(1)} collective-permute-done((bf16[128,1024]{1,0:T(8,128)(2,1)S(1)}, bf16[128,1024]{1,0:T(8,128)(2,1)S(1)}, u32[]{:S(2)}, u32[]{:S(2)}) %collective-permute-start.33) | collective-permute-done | bytes 262176 | tf_op jit(solution)/shard_map/ppermute | solution.py:599
  212.2 8.7 %collective-permute-done.34.refs_2_ = bf16[128,1024]{1,0:T(8,128)(2,1)S(1)} collective-permute-done((bf16[128,1024]{1,0:T(8,128)(2,1)S(1)}, bf16[128,1024]{1,0:T(8,128)(2,1)S(1)}, u32[]{:S(2)}, u32[]{:S(2)}) %collective-permute-start.34) | collective-permute-done | bytes 262176 | tf_op jit(solution)/shard_map/ppermute | solution.py:599
  224.9 5.0 %project_back.1 = (bf16[128,1024]{1,0:T(8,128)(2,1)}, bf16[128,1024]{1,0:T(8,128)(2,1)}, bf16[128,1024]{1,0:T(8,128)(2,1)}, bf16[128,1024]{1,0:T(8,128)(2,1)}, b...) custom-call(s32[3]{0:T(128)} %pad_add_fusion.scalars, bf16[512,256]{1,0:T(8,128)(2,1)} %get-tuple-element.160.dq_ref.query_ref, ...), custom_call_target="tpu_custom_call" | custom-call | flops 805306368 | bytes 4556800 | tf_op jit(solution)/shard_map/project_back/pallas_call | solution.py:39
  229.9 5.1 %last_outer.1 = bf16[8,128,1792]{2,1,0:T(8,128)(2,1)} custom-call(s32[3]{0:T(128)} %pad_add_fusion.scalars, bf16[512,1024]{1,0:T(8,128)(2,1)} %get-tuple-element.171.normed_ref, bf16[512,256]{1,0:T(8,128)(2,1)} %get-tuple-element.160.dq_ref.query_ref, bf16[512,512]{1,0:T(8,128)(2,1)} %get-tuple-element.172.pair_ref, ...), custom_call_target="tpu_custom_call" | custom-call | flops 1073741824 | bytes 6029312 | tf_op jit(solution)/shard_map/last_outer/pallas_call | solution.py:39
  235.0 5.3 %collective-permute-start.38 = (bf16[128,1024]{1,0:T(8,128)(2,1)S(1)}, bf16[128,1024]{1,0:T(8,128)(2,1)S(1)}, u32[]{:S(2)}, u32[]{:S(2)}) collective-permute-start(bf16[128,1024]{1,0:T(8,128)(2,1)S(1)} %copy-done.55), channel_id=1, source_target_pairs={{0,1},{1,0},{2,3},{3,2},{4,5},{5,4},{6,7},{7,6},{8,9},{9,8},{10,11... | collective-permute-start | bytes 786440 | tf_op jit(solution)/shard_map/ppermute | solution.py:599
  241.8 5.6 %collective-permute-done.38.refs_1_ = bf16[128,1024]{1,0:T(8,128)(2,1)S(1)} collective-permute-done((bf16[128,1024]{1,0:T(8,128)(2,1)S(1)}, bf16[128,1024]{1,0:T(8,128)(2,1)S(1)}, u32[]{:S(2)}, u32[]{:S(2)}) %collective-permute-start.38) | collective-permute-done | bytes 262176 | tf_op jit(solution)/shard_map/ppermute | solution.py:599
  254.7 22.4 %collective-permute-done.42.refs_2_ = bf16[128,1024]{1,0:T(8,128)(2,1)S(1)} collective-permute-done((bf16[128,1024]{1,0:T(8,128)(2,1)S(1)}, bf16[128,1024]{1,0:T(8,128)(2,1)S(1)}, u32[]{:S(2)}, u32[]{:S(2)}) %collective-permute-start.42) | collective-permute-done | bytes 262176 | tf_op jit(solution)/shard_map/ppermute | solution.py:599
  277.8 2.8 input_back.1
  282.4 8.7 %collective-permute-start.44 = (bf16[128,1024]{1,0:T(8,128)(2,1)}, bf16[128,1024]{1,0:T(8,128)(2,1)S(1)}, u32[]{:S(2)}, u32[]{:S(2)}) collective-permute-start(bf16[128,1024]{1,0:T(8,128)(2,1)} %get-tuple-element.178.refs_0_), channel_id=1, source_target_pairs={{0,1},{1,0},{2,3},{3,2},{4,5},{5,4},{6,7},{7,6},{8,9},{9,8},{10,11... | collective-permute-start | bytes 786440 | tf_op jit(solution)/shard_map/ppermute | solution.py:599
  299.7 3.5 %collective-permute-start.48 = (bf16[128,256]{1,0:T(8,128)(2,1)}, bf16[128,256]{1,0:T(8,128)(2,1)S(1)}, u32[]{:S(2)}, u32[]{:S(2)}) collective-permute-start(bf16[128,256]{1,0:T(8,128)(2,1)} %get-tuple-element.195), channel_id=1, source_target_pairs={{0,2},{1,3},{2,0},{3,1},{4,6},{5,7},{6,4},{7,5},{8,10},{9,11},{10,... | collective-permute-start | bytes 196616 | tf_op jit(solution)/shard_map/ppermute | solution.py:599
  306.3 9.4 %all-to-all-done.in_ref = f32[32,8,128]{2,1,0:T(8,128)S(1)} async-done(((f32[32,8,128]{2,1,0:T(8,128)}), f32[32,8,128]{2,1,0:T(8,128)S(1)}, u32[]{:S(2)}, u32[]{:S(2)}) %all-to-all-start) | async-done | bytes 131104 | tf_op jit(solution)/shard_map/all_to_all | solution.py:906
  (231 shorter events, 97.8 us)
Async XLA Ops:
  7.2 244.6 %reduce-scatter.3.cloned.1.call-start = ((), (), s32[]{:S(2)}) async-start(), calls=%async_computation.3 | async-start | bytes 4718592 | tf_op jit(solution)/shard_map/reduce_scatter | solution.py:830
  11.9 21.6 %collective-permute-start.1 = (bf16[136,768]{1,0:T(8,128)(2,1)}, bf16[136,768]{1,0:T(8,128)(2,1)S(1)}, u32[]{:S(2)}, u32[]{:S(2)}) collective-permute-start(bf16[136,768]{1,0:T(8,128)(2,1)} %pack.1.refs_0_.refs_2_), channel_id=1, source_target_pairs={{0,16},{4,20},{8,24},{12,28},{16,0},{20,4},{24,8},{28,12},{1,17},{... | collective-permute-start | bytes 626696 | tf_op jit(solution)/shard_map/ppermute | solution.py:593
  17.3 16.3 %collective-permute-start.2 = (bf16[136,768]{1,0:T(8,128)(2,1)S(1)}, bf16[136,768]{1,0:T(8,128)(2,1)S(1)}, u32[]{:S(2)}, u32[]{:S(2)}) collective-permute-start(bf16[136,768]{1,0:T(8,128)(2,1)S(1)} %collective-permute-done.refs_1_.refs_3_), channel_id=1, source_target_pairs={{0,16},{4,20},{8,24},{12,28},{16,0},{20,4},{24,8},{28,12},{1,17},{... | collective-permute-start | bytes 626696 | tf_op jit(solution)/shard_map/ppermute | solution.py:593
  31.5 20.7 %collective-permute-start.16 = (bf16[384,1024]{1,0:T(8,128)(2,1)}, bf16[384,1024]{1,0:T(8,128)(2,1)S(1)}, u32[]{:S(2)}, u32[]{:S(2)}) collective-permute-start(bf16[384,1024]{1,0:T(8,128)(2,1)} %turn.1.refs_4_), channel_id=1, source_target_pairs={{0,8},{4,12},{8,0},{12,4},{16,24},{20,28},{24,16},{28,20},{1,9},{5... | collective-permute-start | bytes 2359304 | tf_op jit(solution)/shard_map/ppermute | solution.py:593
  40.6 20.5 %collective-permute-start.8 = (bf16[512,512]{1,0:T(8,128)(2,1)}, bf16[512,512]{1,0:T(8,128)(2,1)}, u32[]{:S(2)}, u32[]{:S(2)}) collective-permute-start(bf16[512,512]{1,0:T(8,128)(2,1)} %get-tuple-element.109.refs_0_), channel_id=1, source_target_pairs={{0,8},{4,12},{8,0},{12,4},{1,9},{5,13},{9,1},{13,5},{2,10},{6,14},... | collective-permute-start | bytes 1572872 | tf_op jit(solution)/shard_map/ppermute | solution.py:596
  41.1 30.7 %collective-permute-start.17 = (bf16[384,1024]{1,0:T(8,128)(2,1)}, bf16[384,1024]{1,0:T(8,128)(2,1)S(1)}, u32[]{:S(2)}, u32[]{:S(2)}) collective-permute-start(bf16[384,1024]{1,0:T(8,128)(2,1)} %turn.1.refs_4_), channel_id=1, source_target_pairs={{0,16},{4,20},{8,24},{12,28},{16,0},{20,4},{24,8},{28,12},{1,17},{... | collective-permute-start | bytes 2359304 | tf_op jit(solution)/shard_map/ppermute | solution.py:593
  52.2 25.4 %collective-permute-start.18 = (bf16[384,1024]{1,0:T(8,128)(2,1)S(1)}, bf16[384,1024]{1,0:T(8,128)(2,1)S(1)}, u32[]{:S(2)}, u32[]{:S(2)}) collective-permute-start(bf16[384,1024]{1,0:T(8,128)(2,1)S(1)} %collective-permute-done.16.refs_5_), channel_id=1, source_target_pairs={{0,16},{4,20},{8,24},{12,28},{16,0},{20,4},{24,8},{28,12},{1,17},{... | collective-permute-start | bytes 2359304 | tf_op jit(solution)/shard_map/ppermute | solution.py:593
  71.9 22.9 %collective-permute-start.19 = (bf16[384,1024]{1,0:T(8,128)(2,1)S(1)}, bf16[384,1024]{1,0:T(8,128)(2,1)S(1)}, u32[]{:S(2)}, u32[]{:S(2)}) collective-permute-start(bf16[384,1024]{1,0:T(8,128)(2,1)S(1)} %copy-done), channel_id=1, source_target_pairs={{0,4},{4,0},{8,12},{12,8},{1,5},{5,1},{9,13},{13,9},{2,6},{6,2},{1... | collective-permute-start | bytes 2359304 | tf_op jit(solution)/shard_map/ppermute | solution.py:596
  74.7 20.1 %collective-permute-start.20 = (bf16[384,1024]{1,0:T(8,128)(2,1)S(1)}, bf16[384,1024]{1,0:T(8,128)(2,1)S(1)}, u32[]{:S(2)}, u32[]{:S(2)}) collective-permute-start(bf16[384,1024]{1,0:T(8,128)(2,1)S(1)} %collective-permute-done.16.refs_5_), channel_id=1, source_target_pairs={{0,4},{4,0},{8,12},{12,8},{1,5},{5,1},{9,13},{13,9},{2,6},{6,2},{1... | collective-permute-start | bytes 2359304 | tf_op jit(solution)/shard_map/ppermute | solution.py:596
  74.7 20.0 %collective-permute-start.21 = (bf16[384,1024]{1,0:T(8,128)(2,1)S(1)}, bf16[384,1024]{1,0:T(8,128)(2,1)S(1)}, u32[]{:S(2)}, u32[]{:S(2)}) collective-permute-start(bf16[384,1024]{1,0:T(8,128)(2,1)S(1)} %collective-permute-done.17.refs_6_), channel_id=1, source_target_pairs={{0,4},{4,0},{8,12},{12,8},{1,5},{5,1},{9,13},{13,9},{2,6},{6,2},{1... | collective-permute-start | bytes 2359304 | tf_op jit(solution)/shard_map/ppermute | solution.py:596
  77.6 17.2 %collective-permute-start.22 = (bf16[384,1024]{1,0:T(8,128)(2,1)S(1)}, bf16[384,1024]{1,0:T(8,128)(2,1)S(1)}, u32[]{:S(2)}, u32[]{:S(2)}) collective-permute-start(bf16[384,1024]{1,0:T(8,128)(2,1)S(1)} %collective-permute-done.18.refs_7_), channel_id=1, source_target_pairs={{0,4},{4,0},{8,12},{12,8},{1,5},{5,1},{9,13},{13,9},{2,6},{6,2},{1... | collective-permute-start | bytes 2359304 | tf_op jit(solution)/shard_map/ppermute | solution.py:596
  99.8 18.6 %collective-permute-start.23 = (bf16[128,1024]{1,0:T(8,128)(2,1)}, bf16[128,1024]{1,0:T(8,128)(2,1)S(1)}, u32[]{:S(2)}, u32[]{:S(2)}) collective-permute-start(bf16[128,1024]{1,0:T(8,128)(2,1)} %get-tuple-element.127.refs_0_), channel_id=1, source_target_pairs={{0,2},{1,3},{2,0},{3,1},{4,6},{5,7},{6,4},{7,5},{8,10},{9,11},{10,... | collective-permute-start | bytes 786440 | tf_op jit(solution)/shard_map/ppermute | solution.py:599
  99.8 25.4 %collective-permute-start.25 = (bf16[128,1024]{1,0:T(8,128)(2,1)}, bf16[128,1024]{1,0:T(8,128)(2,1)S(1)}, u32[]{:S(2)}, u32[]{:S(2)}) collective-permute-start(bf16[128,1024]{1,0:T(8,128)(2,1)} %get-tuple-element.127.refs_0_), channel_id=1, source_target_pairs={{0,3},{1,2},{2,1},{3,0},{4,7},{5,6},{6,5},{7,4},{8,11},{9,10},{10,... | collective-permute-start | bytes 786440 | tf_op jit(solution)/shard_map/ppermute | solution.py:599
  102.1 23.2 %collective-permute-start.24 = (bf16[128,1024]{1,0:T(8,128)(2,1)}, bf16[128,1024]{1,0:T(8,128)(2,1)S(1)}, u32[]{:S(2)}, u32[]{:S(2)}) collective-permute-start(bf16[128,1024]{1,0:T(8,128)(2,1)} %get-tuple-element.127.refs_0_), channel_id=1, source_target_pairs={{0,1},{1,0},{2,3},{3,2},{4,5},{5,4},{6,7},{7,6},{8,9},{9,8},{10,11... | collective-permute-start | bytes 786440 | tf_op jit(solution)/shard_map/ppermute | solution.py:599
  133.9 22.2 %collective-permute-start.27 = (bf16[128,1024]{1,0:T(8,128)(2,1)S(1)}, bf16[128,1024]{1,0:T(8,128)(2,1)S(1)}, u32[]{:S(2)}, u32[]{:S(2)}) collective-permute-start(bf16[128,1024]{1,0:T(8,128)(2,1)S(1)} %copy-done.54), channel_id=1, source_target_pairs={{0,2},{1,3},{2,0},{3,1},{4,6},{5,7},{6,4},{7,5},{8,10},{9,11},{10,... | collective-permute-start | bytes 786440 | tf_op jit(solution)/shard_map/ppermute | solution.py:599
  133.9 22.2 %collective-permute-start.26 = (bf16[128,1024]{1,0:T(8,128)(2,1)}, bf16[128,1024]{1,0:T(8,128)(2,1)S(1)}, u32[]{:S(2)}, u32[]{:S(2)}) collective-permute-start(bf16[128,1024]{1,0:T(8,128)(2,1)} %get-tuple-element.134), channel_id=1, source_target_pairs={{0,1},{1,0},{2,3},{3,2},{4,5},{5,4},{6,7},{7,6},{8,9},{9,8},{10,11... | collective-permute-start | bytes 786440 | tf_op jit(solution)/shard_map/ppermute | solution.py:599
  160.7 134.6 %reduce-scatter.5.cloned.1.call-start = ((), (), s32[]{:S(2)}) async-start(), calls=%async_computation.4 | async-start | bytes 4128768 | tf_op jit(solution)/shard_map/reduce_scatter | solution.py:844
  179.5 24.4 %collective-permute-start.36 = (bf16[512,512]{1,0:T(8,128)(2,1)}, bf16[512,512]{1,0:T(8,128)(2,1)S(1)}, u32[]{:S(2)}, u32[]{:S(2)}) collective-permute-start(bf16[512,512]{1,0:T(8,128)(2,1)} %get-tuple-element.161), channel_id=1, source_target_pairs={{0,4},{4,0},{8,12},{12,8},{1,5},{5,1},{9,13},{13,9},{2,6},{6,2},{1... | collective-permute-start | bytes 1572872 | tf_op jit(solution)/shard_map/ppermute | solution.py:596
  184.2 39.9 %collective-permute-start.37 = (bf16[512,512]{1,0:T(8,128)(2,1)}, bf16[512,512]{1,0:T(8,128)(2,1)S(1)}, u32[]{:S(2)}, u32[]{:S(2)}) collective-permute-start(bf16[512,512]{1,0:T(8,128)(2,1)} %join.2), channel_id=1, source_target_pairs={{0,8},{4,12},{8,0},{12,4},{1,9},{5,13},{9,1},{13,5},{2,10},{6,14},... | collective-permute-start | bytes 1572872 | tf_op jit(solution)/shard_map/ppermute | solution.py:596
  199.5 21.4 %collective-permute-start.34 = (bf16[128,1024]{1,0:T(8,128)(2,1)S(1)}, bf16[128,1024]{1,0:T(8,128)(2,1)S(1)}, u32[]{:S(2)}, u32[]{:S(2)}) collective-permute-start(bf16[128,1024]{1,0:T(8,128)(2,1)S(1)} %copy-done.49), channel_id=1, source_target_pairs={{0,2},{1,3},{2,0},{3,1},{4,6},{5,7},{6,4},{7,5},{8,10},{9,11},{10,... | collective-permute-start | bytes 786440 | tf_op jit(solution)/shard_map/ppermute | solution.py:599
  201.5 19.4 %collective-permute-start.35 = (bf16[128,1024]{1,0:T(8,128)(2,1)S(1)}, bf16[128,1024]{1,0:T(8,128)(2,1)S(1)}, u32[]{:S(2)}, u32[]{:S(2)}) collective-permute-start(bf16[128,1024]{1,0:T(8,128)(2,1)S(1)} %copy-done.50), channel_id=1, source_target_pairs={{0,3},{1,2},{2,1},{3,0},{4,7},{5,6},{6,5},{7,4},{8,11},{9,10},{10,... | collective-permute-start | bytes 786440 | tf_op jit(solution)/shard_map/ppermute | solution.py:599
  241.8 35.4 %collective-permute-start.42 = (bf16[128,1024]{1,0:T(8,128)(2,1)S(1)}, bf16[128,1024]{1,0:T(8,128)(2,1)S(1)}, u32[]{:S(2)}, u32[]{:S(2)}) collective-permute-start(bf16[128,1024]{1,0:T(8,128)(2,1)S(1)} %copy-done.52), channel_id=1, source_target_pairs={{0,2},{1,3},{2,0},{3,1},{4,6},{5,7},{6,4},{7,5},{8,10},{9,11},{10,... | collective-permute-start | bytes 786440 | tf_op jit(solution)/shard_map/ppermute | solution.py:599
  247.4 34.9 %collective-permute-start.41 = (bf16[128,1024]{1,0:T(8,128)(2,1)S(1)}, bf16[128,1024]{1,0:T(8,128)(2,1)S(1)}, u32[]{:S(2)}, u32[]{:S(2)}) collective-permute-start(bf16[128,1024]{1,0:T(8,128)(2,1)S(1)} %copy-done.8), channel_id=1, source_target_pairs={{0,3},{1,2},{2,1},{3,0},{4,7},{5,6},{6,5},{7,4},{8,11},{9,10},{10,... | collective-permute-start | bytes 786440 | tf_op jit(solution)/shard_map/ppermute | solution.py:599
  248.5 51.1 %collective-permute-start.40 = (bf16[128,1024]{1,0:T(8,128)(2,1)S(1)}, bf16[128,1024]{1,0:T(8,128)(2,1)S(1)}, u32[]{:S(2)}, u32[]{:S(2)}) collective-permute-start(bf16[128,1024]{1,0:T(8,128)(2,1)S(1)} %copy-done.8), channel_id=1, source_target_pairs={{0,2},{1,3},{2,0},{3,1},{4,6},{5,7},{6,4},{7,5},{8,10},{9,11},{10,... | collective-permute-start | bytes 786440 | tf_op jit(solution)/shard_map/ppermute | solution.py:599
  251.0 48.7 %collective-permute-start.39 = (bf16[128,1024]{1,0:T(8,128)(2,1)S(1)}, bf16[128,1024]{1,0:T(8,128)(2,1)S(1)}, u32[]{:S(2)}, u32[]{:S(2)}) collective-permute-start(bf16[128,1024]{1,0:T(8,128)(2,1)S(1)} %copy-done.8), channel_id=1, source_target_pairs={{0,1},{1,0},{2,3},{3,2},{4,5},{5,4},{6,7},{7,6},{8,9},{9,8},{10,11... | collective-permute-start | bytes 786440 | tf_op jit(solution)/shard_map/ppermute | solution.py:599
  280.6 22.5 %collective-permute-start.46 = (bf16[128,1024]{1,0:T(8,128)(2,1)}, bf16[128,1024]{1,0:T(8,128)(2,1)S(1)}, u32[]{:S(2)}, u32[]{:S(2)}) collective-permute-start(bf16[128,1024]{1,0:T(8,128)(2,1)} %get-tuple-element.178.refs_0_), channel_id=1, source_target_pairs={{0,3},{1,2},{2,1},{3,0},{4,7},{5,6},{6,5},{7,4},{8,11},{9,10},{10,... | collective-permute-start | bytes 786440 | tf_op jit(solution)/shard_map/ppermute | solution.py:599
  282.4 35.5 %collective-permute-start.45 = (bf16[128,1024]{1,0:T(8,128)(2,1)}, bf16[128,1024]{1,0:T(8,128)(2,1)S(1)}, u32[]{:S(2)}, u32[]{:S(2)}) collective-permute-start(bf16[128,1024]{1,0:T(8,128)(2,1)} %get-tuple-element.178.refs_0_), channel_id=1, source_target_pairs={{0,2},{1,3},{2,0},{3,1},{4,6},{5,7},{6,4},{7,5},{8,10},{9,11},{10,... | collective-permute-start | bytes 786440 | tf_op jit(solution)/shard_map/ppermute | solution.py:599
  282.4 35.5 %collective-permute-start.44 = (bf16[128,1024]{1,0:T(8,128)(2,1)}, bf16[128,1024]{1,0:T(8,128)(2,1)S(1)}, u32[]{:S(2)}, u32[]{:S(2)}) collective-permute-start(bf16[128,1024]{1,0:T(8,128)(2,1)} %get-tuple-element.178.refs_0_), channel_id=1, source_target_pairs={{0,1},{1,0},{2,3},{3,2},{4,5},{5,4},{6,7},{7,6},{8,9},{9,8},{10,11... | collective-permute-start | bytes 786440 | tf_op jit(solution)/shard_map/ppermute | solution.py:599
  292.7 23.0 %all-to-all-start = ((f32[32,8,128]{2,1,0:T(8,128)}), f32[32,8,128]{2,1,0:T(8,128)S(1)}, u32[]{:S(2)}, u32[]{:S(2)}) async-start(f32[32,8,128]{2,1,0:T(8,128)} %small.1), calls=%async_computation.1 | async-start | bytes 262144 | tf_op jit(solution)/shard_map/all_to_all | solution.py:906
  299.6 22.0 %collective-permute-start.47 = (bf16[128,256]{1,0:T(8,128)(2,1)}, bf16[128,256]{1,0:T(8,128)(2,1)S(1)}, u32[]{:S(2)}, u32[]{:S(2)}) collective-permute-start(bf16[128,256]{1,0:T(8,128)(2,1)} %get-tuple-element.194), channel_id=1, source_target_pairs={{0,1},{1,0},{2,3},{3,2},{4,5},{5,4},{6,7},{7,6},{8,9},{9,8},{10,11... | collective-permute-start | bytes 196616 | tf_op jit(solution)/shard_map/ppermute | solution.py:599
  299.7 21.9 %collective-permute-start.48 = (bf16[128,256]{1,0:T(8,128)(2,1)}, bf16[128,256]{1,0:T(8,128)(2,1)S(1)}, u32[]{:S(2)}, u32[]{:S(2)}) collective-permute-start(bf16[128,256]{1,0:T(8,128)(2,1)} %get-tuple-element.195), channel_id=1, source_target_pairs={{0,2},{1,3},{2,0},{3,1},{4,6},{5,7},{6,4},{7,5},{8,10},{9,11},{10,... | collective-permute-start | bytes 196616 | tf_op jit(solution)/shard_map/ppermute | solution.py:599
  303.1 18.5 %collective-permute-start.49 = (bf16[128,256]{1,0:T(8,128)(2,1)}, bf16[128,256]{1,0:T(8,128)(2,1)S(1)}, u32[]{:S(2)}, u32[]{:S(2)}) collective-permute-start(bf16[128,256]{1,0:T(8,128)(2,1)} %get-tuple-element.196), channel_id=1, source_target_pairs={{0,3},{1,2},{2,1},{3,0},{4,7},{5,6},{6,5},{7,4},{8,11},{9,10},{10,... | collective-permute-start | bytes 196616 | tf_op jit(solution)/shard_map/ppermute | solution.py:599
  (83 other events, 657.2 us)
Sparse Core Ops, SparseCore 0:
  160.9 58.0 reduce-scatter.2
  235.1 49.7 reduce-scatter.4
